TPU v7x, 32 devices: a whole 2x2x4 slice. The times are simulated.
32 devices in a mesh: frame: 4 (over y, x), vox: 8 (over z, core).
Axes of the slice: x: 2, y: 2, z: 4, core: 2. Of those that a mesh axis runs over, the one named last changes fastest.
Arguments:
- pool: bfloat16 [2048, 8192], P('frame', 'vox'), may hold values from -6 to 6
- dictionary: bfloat16 [1024, 8192], P(None, 'vox'), may hold values from -0.13258252 to 0.13258252
- support: int32 [1024, 64], P(None, 'vox'), may hold values from 0 to 1, as said below
- pick: int32 [1024], P('frame'), may hold values from 0 to 511
Outputs:
- codes: bfloat16 [1024, 1024], P('frame')
- gradient: float32 [1024, 8192], P('frame', 'vox')
Inputs may be any that keep to these rules, and one draw needn't show every extreme that they name: Every mode has at least one voxel block in its support.
All inputs are finite; a program needn't handle non-finite values.
Results may differ from a plain program's by a relative error of at most 0.015.
Values may be sent and summed in bfloat16 or wider, within the bound.
No kernel may reach another device: no remote copies, remote signals or barrier semaphores. Data moves between devices by JAX's collectives and lax.ppermute only.
A program may use at most 64 MiB of HBM per device.

v0:
```python
import functools

import jax
import jax.numpy as jnp
from jax import lax
from jax.experimental import pallas as pl
from jax.experimental.pallas import tpu as pltpu
from jax.sharding import PartitionSpec as P


LANE = 128
EXTRA = 16
BF = jnp.bfloat16
F32 = jnp.float32


def mm(left, right, a, b):
    return lax.dot_general(left, right, (((a,), (b,)), ((), ())), preferred_element_type=F32)


def shrink(value, limit):
    return value - jnp.clip(value, -limit, limit)


def expand_keep(sup, width):
    blocks = sup.shape[0]
    row = lax.broadcasted_iota(jnp.int32, (blocks, width), 0)
    col = lax.broadcasted_iota(jnp.int32, (blocks, width), 1)
    spread = jnp.where(col // (width // blocks) == row, 1.0, 0.0).astype(BF)
    return mm(sup.astype(F32).astype(BF), spread, 0, 0).astype(BF)


def split_rows(total):
    hi = total.astype(BF)
    rest = total - hi.astype(F32)
    mid = rest.astype(BF)
    low = (rest - mid.astype(F32)).astype(BF)
    row = lax.broadcasted_iota(jnp.int32, (EXTRA, LANE), 0)
    out = jnp.where(row == 0, hi.astype(F32), 0.0)
    out = jnp.where(row == 1, mid.astype(F32), out)
    return jnp.where(row == 2, low.astype(F32), out)


def block_of(index, size):
    return pl.ds(pl.multiple_of(index * size, size), size)


def prepare(pool, dic, sup, pick, batch, masked, keep, send, lhs):
    v, f = lax.axis_index("vox"), lax.axis_index("frame")
    frames, width = batch.shape
    modes = dic.shape[0]
    own = lhs.shape[0] - frames
    source = lax.broadcasted_iota(jnp.int32, (pool.shape[0], frames), 0)
    chosen = jnp.where(source == pick[...], 1.0, 0.0).astype(BF)
    rows = mm(chosen, pool[...], 0, 0).astype(BF)
    batch[...] = rows
    lhs[:frames, :] = rows
    for m in range(modes // LANE):
        at = slice(m * LANE, (m + 1) * LANE)
        masked[at, :] = dic[at, :] * expand_keep(sup[:, at], width)
    lhs[frames:, :] = masked[block_of(f, own), :]
    ones = jnp.ones((8, width), BF)
    for r in range(modes // LANE):
        block = masked[block_of((v % (modes // LANE)) ^ r, LANE), :]
        part = mm(lhs[...], block, 1, 1)
        square = jnp.square(block.astype(F32))
        hi = square.astype(BF)
        lo = (square - hi.astype(F32)).astype(BF)
        energy = (mm(ones, hi, 1, 1) + mm(ones, lo, 1, 1))[:1]
        height = part.shape[0]
        if r % 2:
            send[r // 2, :height, :] = part.astype(BF)
            send[r // 2, height:, :] = split_rows(energy).astype(BF)
        else:
            row = lax.broadcasted_iota(jnp.int32, (EXTRA, LANE), 0)
            keep[r // 2, :height, :] = part
            keep[r // 2, height:, :] = jnp.where(row == 0, energy, 0.0)


def fold_core(keep, got, own, *sends):
    height = own.shape[0] - EXTRA
    own[...] = keep[0] + got[0].astype(F32)
    for i, out in enumerate(sends):
        total = keep[i + 1] + got[i + 1].astype(F32)
        out[:height, :] = total[:height].astype(BF)
        out[height:, :] = split_rows(jnp.sum(total[height:], axis=0, keepdims=True)).astype(BF)


def fold_line(own, *rest):
    *gots, first, corr, step, gram = rest
    frames = first.shape[0]
    total = own[...]
    for got in gots:
        total = total + got[...].astype(F32)
    energy = jnp.sum(total[total.shape[0] - EXTRA :], axis=0, keepdims=True)
    scale = 1.0 / (energy + 1e-05)
    corr[...] = total[:frames]
    first[...] = shrink(total[:frames] * scale, 0.3 * scale).astype(BF)
    step[...] = jnp.broadcast_to(scale, step.shape)
    gram[...] = total[frames : total.shape[0] - EXTRA].astype(BF)


def second(n_first, n_gram, *refs):
    firsts = refs[:n_first]
    grams = refs[n_first : n_first + n_gram]
    corr, step, codes, square = refs[n_first + n_gram :]
    v, f = lax.axis_index("vox"), lax.axis_index("frame")
    own = grams[0].shape[0]
    for s in range(n_gram):
        square[block_of(f ^ s, own), :] = grams[s][...]
    push = -corr[...]
    for r in range(n_first):
        push = push + mm(firsts[r][...], square[block_of((v % n_first) ^ r, LANE), :], 1, 0)
    scale = step[:1, :]
    codes[...] = shrink(firsts[0][...].astype(F32) - scale * push, 0.3 * scale).astype(BF)


def pack(*refs):
    *parts, out = refs
    for i, part in enumerate(parts):
        out[i] = part[...]


def place(half, other, whole):
    v = lax.axis_index("vox")
    count = half.shape[0]
    for i in range(count):
        whole[:, block_of((v % (2 * count)) ^ (2 * i), LANE)] = half[i]
        whole[:, block_of((v % (2 * count)) ^ (2 * i + 1), LANE)] = other[i]


def own_group(half, other, masked, batch, codes, total):
    f = lax.axis_index("frame")
    place(half, other, codes)
    error = (mm(codes[...], masked[...], 1, 0) - batch[...].astype(F32)).astype(BF)
    rows = total.shape[0]
    total[...] = mm(codes[:, block_of(f, rows)], error, 0, 0)


def last_groups(n, scale, *refs):
    halves, others, batches = refs[:n], refs[n : 2 * n], refs[2 * n : 3 * n]
    masked, sup, total, gradient, codes = refs[3 * n :]
    f = lax.axis_index("frame")
    rows = total.shape[0]
    acc = total[...]
    for i in range(n):
        place(halves[i], others[i], codes)
        error = (mm(codes[...], masked[...], 1, 0) - batches[i][...].astype(F32)).astype(BF)
        acc = acc + mm(codes[:, block_of(f, rows)], error, 0, 0)
    kept = expand_keep(sup[:, block_of(f, rows)], total.shape[1]).astype(F32)
    gradient[...] = kept * acc * scale


def call(kernel, outs, args, scratch=(), flops=0):
    moved = sum(a.size * a.dtype.itemsize for a in (*args, *outs))
    single = len(outs) == 1
    return pl.pallas_call(
        kernel,
        out_shape=outs[0] if single else outs,
        in_specs=[pl.BlockSpec(memory_space=pltpu.VMEM)] * len(args),
        out_specs=pl.BlockSpec(memory_space=pltpu.VMEM)
        if single
        else [pl.BlockSpec(memory_space=pltpu.VMEM)] * len(outs),
        scratch_shapes=list(scratch),
        compiler_params=pltpu.CompilerParams(vmem_limit_bytes=8 * 2**20),
        cost_estimate=pl.CostEstimate(flops=flops, bytes_accessed=moved, transcendentals=0),
    )(*args)


def shape(dims, dtype):
    return jax.ShapeDtypeStruct(dims, dtype)


def work(pool, dictionary, support, pick):
    n_vox, n_frame = lax.axis_size("vox"), lax.axis_size("frame")
    modes, width = dictionary.shape
    frames = pick.shape[0]
    blocks = modes // LANE
    own = modes // n_frame
    height = frames + own + EXTRA
    line = [m for m in range(2, blocks, 2)]

    def hop(x, axis, m):
        n = n_vox if axis == "vox" else n_frame
        return lax.ppermute(x, axis, [(k, k ^ m) for k in range(n)])

    sup = support.T
    batch, masked, keep, send = call(
        prepare,
        [
            shape((frames, width), BF),
            shape((modes, width), BF),
            shape((blocks // 2, height, LANE), F32),
            shape((blocks // 2, height, LANE), BF),
        ],
        (pool, dictionary, sup, pick.reshape(1, frames)),
        [pltpu.VMEM((frames + own, width), BF)],
        2 * (frames + own) * modes * width,
    )
    got = hop(send, "vox", 1)
    mine, *sends = call(
        fold_core,
        [shape((height, LANE), F32)] + [shape((height, LANE), BF)] * len(line),
        (keep, got),
    )
    gots = [hop(s, "vox", m) for s, m in zip(sends, line)]
    far = blocks
    while far < n_vox:
        total = mine
        for g in gots:
            total = total + g.astype(F32)
        top, end = total[:-EXTRA].astype(BF), jnp.sum(total[-EXTRA:], 0, keepdims=True)
        sent = jnp.concatenate([top, split_rows(end).astype(BF)], 0)
        mine, gots = sent.astype(F32), [hop(sent, "vox", far)]
        far *= 2
    first, corr, step, gram = call(
        fold_line,
        [
            shape((frames, LANE), BF),
            shape((frames, LANE), F32),
            shape((8, LANE), F32),
            shape((own, LANE), BF),
        ],
        (mine, *gots),
    )
    firsts = [first] + [hop(first, "vox", m) for m in line]
    grams = [gram] + [hop(gram, "frame", s) for s in range(1, n_frame)]
    odd = [hop(x, "vox", 1) for x in firsts]
    ordered = [x for pair in zip(firsts, odd) for x in pair]
    code = call(
        functools.partial(second, blocks, n_frame),
        [shape((frames, LANE), BF)],
        (*ordered, *grams, corr, step),
        [pltpu.VMEM((modes, LANE), BF)],
        2 * frames * modes * LANE,
    )
    half = call(
        pack, [shape((blocks // 2, frames, LANE), BF)], (code, *[hop(code, "vox", m) for m in line])
    )
    batches = [hop(batch, "frame", s) for s in range(1, n_frame)]
    halves = [hop(half, "frame", s) for s in range(1, n_frame)]
    other = hop(half, "vox", 1)
    others = [hop(h, "vox", 1) for h in halves]
    codes, total = call(
        own_group,
        [shape((frames, modes), BF), shape((own, width), F32)],
        (half, other, masked, batch),
        flops=2 * frames * modes * width,
    )
    gradient = call(
        functools.partial(last_groups, n_frame - 1, 1.0 / (frames * n_frame)),
        [shape((own, width), F32)],
        (*halves, *others, *batches, masked, sup, total),
        [pltpu.VMEM((frames, modes), BF)],
        2 * (n_frame - 1) * frames * modes * width,
    )
    return codes, gradient


def solution(mesh):
    placed = (P("frame", "vox"), P(None, "vox"), P(None, "vox"), P("frame"))
    return jax.shard_map(
        work,
        mesh=mesh,
        in_specs=placed,
        out_specs=(P("frame", None), P("frame", "vox")),
        check_vma=False,
    )
```

profile of v0, /device:TPU:0, one launch (start us, length us, event | category | flops | bytes accessed | tf_op | source)
XLA Modules:
  0.0 100.5 jit_solution(14467866749481037997)
XLA Ops:
  1.4 1.6 %copy-done.1 = bf16[1024,1024]{1,0:T(8,128)(2,1)S(1)} copy-done((bf16[1024,1024]{1,0:T(8,128)(2,1)S(1)}, bf16[1024,1024]{1,0:T(8,128)(2,1)}, u32[]{:S(2)}) %copy-start.1) | copy-done | bytes 2097176
  3.0 1.2 %copy-done.2 = bf16[512,1024]{1,0:T(8,128)(2,1)S(1)} copy-done((bf16[512,1024]{1,0:T(8,128)(2,1)S(1)}, bf16[512,1024]{1,0:T(8,128)(2,1)}, u32[]{:S(2)}) %copy-start.2) | copy-done | bytes 1048600
  4.9 4.5 %shard_map.59 = (bf16[256,1024]{1,0:T(8,128)(2,1)S(1)}, bf16[1024,1024]{1,0:T(8,128)(2,1)S(1)}, f32[4,528,128]{2,1,0:T(8,128)S(1)}, bf16[4,528,128]{2,1,0:T(8,128)(2,1)S(1)}) custom-call(bf16[512,1024]{1,0:T(8,128)(2,1)S(1)} %copy-done.2, bf16[1024,1024]{1,0:T(8,128)(2,1)S(1)} %copy-done.1, s32[8,1024]{1,0:T(8,128)S(1)} %bitcast.2, s32[1,256]{1,0:T(1,128)S(1)} %bitcast.4), custom_call_target="tpu_custom_call" | custom-call | flops 1073741824 | bytes 7422976 | tf_op jit(solution)/shard_map/pallas_call | solution.py:157
  9.9 1.6 %collective-permute-done.got = bf16[4,528,128]{2,1,0:T(8,128)(2,1)S(1)} collective-permute-done((bf16[4,528,128]{2,1,0:T(8,128)(2,1)S(1)}, bf16[4,528,128]{2,1,0:T(8,128)(2,1)S(1)}, u32[]{:S(2)}, u32[]{:S(2)}) %collective-permute-start) | collective-permute-done | bytes 540704 | tf_op jit(solution)/shard_map/ppermute | solution.py:185
  11.6 3.0 %collective-permute-start.1 = (bf16[528,128]{1,0:T(8,128)(2,1)S(1)}, bf16[528,128]{1,0:T(8,128)(2,1)S(1)}, u32[]{:S(2)}, u32[]{:S(2)}) collective-permute-start(bf16[528,128]{1,0:T(8,128)(2,1)S(1)} %get-tuple-element.19), channel_id=1, source_target_pairs={{0,2},{1,3},{2,0},{3,1},{4,6},{5,7},{6,4},{7,5},{8,10},{9,11},{10,... | collective-permute-start | bytes 405512 | tf_op jit(solution)/shard_map/ppermute | solution.py:185
  14.6 2.6 %collective-permute-start.2 = (bf16[528,128]{1,0:T(8,128)(2,1)S(1)}, bf16[528,128]{1,0:T(8,128)(2,1)S(1)}, u32[]{:S(2)}, u32[]{:S(2)}) collective-permute-start(bf16[528,128]{1,0:T(8,128)(2,1)S(1)} %get-tuple-element.20), channel_id=1, source_target_pairs={{0,4},{1,5},{2,6},{3,7},{4,0},{5,1},{6,2},{7,3},{8,12},{9,13},{10,... | collective-permute-start | bytes 405512 | tf_op jit(solution)/shard_map/ppermute | solution.py:185
  17.2 3.3 %collective-permute-done.1.rest_0_ = bf16[528,128]{1,0:T(8,128)(2,1)S(1)} collective-permute-done((bf16[528,128]{1,0:T(8,128)(2,1)S(1)}, bf16[528,128]{1,0:T(8,128)(2,1)S(1)}, u32[]{:S(2)}, u32[]{:S(2)}) %collective-permute-start.1) | collective-permute-done | bytes 135200 | tf_op jit(solution)/shard_map/ppermute | solution.py:185
  20.5 7.3 %collective-permute-done.2.rest_1_ = bf16[528,128]{1,0:T(8,128)(2,1)S(1)} collective-permute-done((bf16[528,128]{1,0:T(8,128)(2,1)S(1)}, bf16[528,128]{1,0:T(8,128)(2,1)S(1)}, u32[]{:S(2)}, u32[]{:S(2)}) %collective-permute-start.2) | collective-permute-done | bytes 135200 | tf_op jit(solution)/shard_map/ppermute | solution.py:185
  27.9 2.5 %collective-permute-start.5 = (bf16[256,128]{1,0:T(8,128)(2,1)S(1)}, bf16[256,128]{1,0:T(8,128)(2,1)S(1)}, u32[]{:S(2)}, u32[]{:S(2)}) collective-permute-start(bf16[256,128]{1,0:T(8,128)(2,1)S(1)} %get-tuple-element.22.refs_0_), channel_id=1, source_target_pairs={{0,2},{1,3},{2,0},{3,1},{4,6},{5,7},{6,4},{7,5},{8,10},{9,11},{10,... | collective-permute-start | bytes 196616 | tf_op jit(solution)/shard_map/ppermute | solution.py:185
  30.4 1.5 %collective-permute-start.24 = (bf16[256,1024]{1,0:T(8,128)(2,1)S(1)}, bf16[256,1024]{1,0:T(8,128)(2,1)S(1)}, u32[]{:S(2)}, u32[]{:S(2)}) collective-permute-start(bf16[256,1024]{1,0:T(8,128)(2,1)S(1)} %get-tuple-element.27.batch), channel_id=1, source_target_pairs={{0,8},{8,0},{16,24},{24,16},{1,9},{9,1},{17,25},{25,17},{2,10},{10... | collective-permute-start | bytes 1572872 | tf_op jit(solution)/shard_map/ppermute | solution.py:185
  33.0 1.4 %collective-permute-start.9 = (bf16[256,128]{1,0:T(8,128)(2,1)S(1)}, bf16[256,128]{1,0:T(8,128)(2,1)S(1)}, u32[]{:S(2)}, u32[]{:S(2)}) collective-permute-start(bf16[256,128]{1,0:T(8,128)(2,1)S(1)} %get-tuple-element.22.refs_0_), channel_id=1, source_target_pairs={{0,6},{1,7},{2,4},{3,5},{4,2},{5,3},{6,0},{7,1},{8,14},{9,15},{10,... | collective-permute-start | bytes 196616 | tf_op jit(solution)/shard_map/ppermute | solution.py:185
  34.9 1.5 %collective-permute-start.12 = (bf16[256,128]{1,0:T(8,128)(2,1)S(1)}, bf16[256,128]{1,0:T(8,128)(2,1)S(1)}, u32[]{:S(2)}, u32[]{:S(2)}) collective-permute-start(bf16[256,128]{1,0:T(8,128)(2,1)S(1)} %get-tuple-element.23.refs_8_), channel_id=1, source_target_pairs={{0,16},{8,24},{16,0},{24,8},{1,17},{9,25},{17,1},{25,9},{2,18},{10... | collective-permute-start | bytes 196616 | tf_op jit(solution)/shard_map/ppermute | solution.py:185
  36.4 3.2 %collective-permute-done.7.refs_4_ = bf16[256,128]{1,0:T(8,128)(2,1)S(1)} collective-permute-done((bf16[256,128]{1,0:T(8,128)(2,1)S(1)}, bf16[256,128]{1,0:T(8,128)(2,1)S(1)}, u32[]{:S(2)}, u32[]{:S(2)}) %collective-permute-start.7) | collective-permute-done | bytes 65568 | tf_op jit(solution)/shard_map/ppermute | solution.py:185
  39.6 2.0 %collective-permute-start.13 = (bf16[256,128]{1,0:T(8,128)(2,1)S(1)}, bf16[256,128]{1,0:T(8,128)(2,1)S(1)}, u32[]{:S(2)}, u32[]{:S(2)}) collective-permute-start(bf16[256,128]{1,0:T(8,128)(2,1)S(1)} %get-tuple-element.23.refs_8_), channel_id=1, source_target_pairs={{0,24},{8,16},{16,8},{24,0},{1,25},{9,17},{17,9},{25,1},{2,26},{10... | collective-permute-start | bytes 196616 | tf_op jit(solution)/shard_map/ppermute | solution.py:185
  41.6 4.9 %collective-permute-done.11.refs_9_ = bf16[256,128]{1,0:T(8,128)(2,1)S(1)} collective-permute-done((bf16[256,128]{1,0:T(8,128)(2,1)S(1)}, bf16[256,128]{1,0:T(8,128)(2,1)S(1)}, u32[]{:S(2)}, u32[]{:S(2)}) %collective-permute-start.11) | collective-permute-done | bytes 65568 | tf_op jit(solution)/shard_map/ppermute | solution.py:185
  48.8 2.8 %collective-permute-start.15 = (bf16[256,128]{1,0:T(8,128)(2,1)S(1)}, bf16[256,128]{1,0:T(8,128)(2,1)S(1)}, u32[]{:S(2)}, u32[]{:S(2)}) collective-permute-start(bf16[256,128]{1,0:T(8,128)(2,1)S(1)} %shard_map.62.refs_0_), channel_id=1, source_target_pairs={{0,4},{1,5},{2,6},{3,7},{4,0},{5,1},{6,2},{7,3},{8,12},{9,13},{10,... | collective-permute-start | bytes 196616 | tf_op jit(solution)/shard_map/ppermute | solution.py:185
  51.6 1.4 %collective-permute-start.16 = (bf16[256,128]{1,0:T(8,128)(2,1)S(1)}, bf16[256,128]{1,0:T(8,128)(2,1)S(1)}, u32[]{:S(2)}, u32[]{:S(2)}) collective-permute-start(bf16[256,128]{1,0:T(8,128)(2,1)S(1)} %shard_map.62.refs_0_), channel_id=1, source_target_pairs={{0,6},{1,7},{2,4},{3,5},{4,2},{5,3},{6,0},{7,1},{8,14},{9,15},{10,... | collective-permute-start | bytes 196616 | tf_op jit(solution)/shard_map/ppermute | solution.py:185
  53.7 3.0 %collective-permute-done.15.refs_2_ = bf16[256,128]{1,0:T(8,128)(2,1)S(1)} collective-permute-done((bf16[256,128]{1,0:T(8,128)(2,1)S(1)}, bf16[256,128]{1,0:T(8,128)(2,1)S(1)}, u32[]{:S(2)}, u32[]{:S(2)}) %collective-permute-start.15) | collective-permute-done | bytes 65568 | tf_op jit(solution)/shard_map/ppermute | solution.py:185
  57.9 1.2 %collective-permute-start.25 = (bf16[256,1024]{1,0:T(8,128)(2,1)S(1)}, bf16[256,1024]{1,0:T(8,128)(2,1)S(1)}, u32[]{:S(2)}, u32[]{:S(2)}) collective-permute-start(bf16[256,1024]{1,0:T(8,128)(2,1)S(1)} %get-tuple-element.27.batch), channel_id=1, source_target_pairs={{0,16},{8,24},{16,0},{24,8},{1,17},{9,25},{17,1},{25,9},{2,18},{10... | collective-permute-start | bytes 1572872 | tf_op jit(solution)/shard_map/ppermute | solution.py:185
  59.1 1.8 %collective-permute-start.26 = (bf16[256,1024]{1,0:T(8,128)(2,1)S(1)}, bf16[256,1024]{1,0:T(8,128)(2,1)S(1)}, u32[]{:S(2)}, u32[]{:S(2)}) collective-permute-start(bf16[256,1024]{1,0:T(8,128)(2,1)S(1)} %get-tuple-element.27.batch), channel_id=1, source_target_pairs={{0,24},{8,16},{16,8},{24,0},{1,25},{9,17},{17,9},{25,1},{2,26},{10... | collective-permute-start | bytes 1572872 | tf_op jit(solution)/shard_map/ppermute | solution.py:185
  62.6 1.8 %collective-permute-start.20 = (bf16[4,256,128]{2,1,0:T(8,128)(2,1)S(1)}, bf16[4,256,128]{2,1,0:T(8,128)(2,1)S(1)}, u32[]{:S(2)}, u32[]{:S(2)}) collective-permute-start(bf16[4,256,128]{2,1,0:T(8,128)(2,1)S(1)} %shard_map.63.half), channel_id=1, source_target_pairs={{0,24},{8,16},{16,8},{24,0},{1,25},{9,17},{17,9},{25,1},{2,26},{10... | collective-permute-start | bytes 786440 | tf_op jit(solution)/shard_map/ppermute | solution.py:185
  64.4 15.5 %collective-permute-done.18.refs_0_ = bf16[4,256,128]{2,1,0:T(8,128)(2,1)S(1)} collective-permute-done((bf16[4,256,128]{2,1,0:T(8,128)(2,1)S(1)}, bf16[4,256,128]{2,1,0:T(8,128)(2,1)S(1)}, u32[]{:S(2)}, u32[]{:S(2)}) %collective-permute-start.18) | collective-permute-done | bytes 262176 | tf_op jit(solution)/shard_map/ppermute | solution.py:185
  79.9 14.8 %collective-permute-done.19.refs_1_ = bf16[4,256,128]{2,1,0:T(8,128)(2,1)S(1)} collective-permute-done((bf16[4,256,128]{2,1,0:T(8,128)(2,1)S(1)}, bf16[4,256,128]{2,1,0:T(8,128)(2,1)S(1)}, u32[]{:S(2)}, u32[]{:S(2)}) %collective-permute-start.19) | collective-permute-done | bytes 262176 | tf_op jit(solution)/shard_map/ppermute | solution.py:185
  96.6 3.9 %shard_map.65 = f32[256,1024]{1,0:T(8,128)} custom-call(bf16[4,256,128]{2,1,0:T(8,128)(2,1)S(1)} %collective-permute-done.18.refs_0_, bf16[4,256,128]{2,1,0:T(8,128)(2,1)S(1)} %collective-permute-done.19.refs_1_, bf16[4,256,128]{2,1,0:T(8,128)(2,1)S(1)} %collective-permute-done.20.refs_2_, bf16[4,256,128]{2,1,0:T(8,128)(2,1)S(1)} %collective-permute-done.21.refs_3_, ...), custom_call_target="tpu_custom_call" | custom-call | flops 1610612736 | bytes 7372800 | tf_op jit(solution)/shard_map/pallas_call | solution.py:157
  (45 shorter events, 11.7 us)
Async XLA Ops:
  9.4 2.1 %collective-permute-start = (bf16[4,528,128]{2,1,0:T(8,128)(2,1)S(1)}, bf16[4,528,128]{2,1,0:T(8,128)(2,1)S(1)}, u32[]{:S(2)}, u32[]{:S(2)}) collective-permute-start(bf16[4,528,128]{2,1,0:T(8,128)(2,1)S(1)} %get-tuple-element.17), channel_id=1, source_target_pairs={{0,1},{1,0},{2,3},{3,2},{4,5},{5,4},{6,7},{7,6},{8,9},{9,8},{10,11... | collective-permute-start | bytes 1622024 | tf_op jit(solution)/shard_map/ppermute | solution.py:185
  11.6 8.9 %collective-permute-start.1 = (bf16[528,128]{1,0:T(8,128)(2,1)S(1)}, bf16[528,128]{1,0:T(8,128)(2,1)S(1)}, u32[]{:S(2)}, u32[]{:S(2)}) collective-permute-start(bf16[528,128]{1,0:T(8,128)(2,1)S(1)} %get-tuple-element.19), channel_id=1, source_target_pairs={{0,2},{1,3},{2,0},{3,1},{4,6},{5,7},{6,4},{7,5},{8,10},{9,11},{10,... | collective-permute-start | bytes 405512 | tf_op jit(solution)/shard_map/ppermute | solution.py:185
  14.6 13.2 %collective-permute-start.2 = (bf16[528,128]{1,0:T(8,128)(2,1)S(1)}, bf16[528,128]{1,0:T(8,128)(2,1)S(1)}, u32[]{:S(2)}, u32[]{:S(2)}) collective-permute-start(bf16[528,128]{1,0:T(8,128)(2,1)S(1)} %get-tuple-element.20), channel_id=1, source_target_pairs={{0,4},{1,5},{2,6},{3,7},{4,0},{5,1},{6,2},{7,3},{8,12},{9,13},{10,... | collective-permute-start | bytes 405512 | tf_op jit(solution)/shard_map/ppermute | solution.py:185
  17.2 10.6 %collective-permute-start.3 = (bf16[528,128]{1,0:T(8,128)(2,1)S(1)}, bf16[528,128]{1,0:T(8,128)(2,1)S(1)}, u32[]{:S(2)}, u32[]{:S(2)}) collective-permute-start(bf16[528,128]{1,0:T(8,128)(2,1)S(1)} %get-tuple-element.21), channel_id=1, source_target_pairs={{0,6},{1,7},{2,4},{3,5},{4,2},{5,3},{6,0},{7,1},{8,14},{9,15},{10,... | collective-permute-start | bytes 405512 | tf_op jit(solution)/shard_map/ppermute | solution.py:185
  27.9 6.5 %collective-permute-start.4 = (bf16[256,128]{1,0:T(8,128)(2,1)S(1)}, bf16[256,128]{1,0:T(8,128)(2,1)S(1)}, u32[]{:S(2)}, u32[]{:S(2)}) collective-permute-start(bf16[256,128]{1,0:T(8,128)(2,1)S(1)} %get-tuple-element.22.refs_0_), channel_id=1, source_target_pairs={{0,1},{1,0},{2,3},{3,2},{4,5},{5,4},{6,7},{7,6},{8,9},{9,8},{10,11... | collective-permute-start | bytes 196616 | tf_op jit(solution)/shard_map/ppermute | solution.py:185
  27.9 7.0 %collective-permute-start.5 = (bf16[256,128]{1,0:T(8,128)(2,1)S(1)}, bf16[256,128]{1,0:T(8,128)(2,1)S(1)}, u32[]{:S(2)}, u32[]{:S(2)}) collective-permute-start(bf16[256,128]{1,0:T(8,128)(2,1)S(1)} %get-tuple-element.22.refs_0_), channel_id=1, source_target_pairs={{0,2},{1,3},{2,0},{3,1},{4,6},{5,7},{6,4},{7,5},{8,10},{9,11},{10,... | collective-permute-start | bytes 196616 | tf_op jit(solution)/shard_map/ppermute | solution.py:185
  30.4 31.0 %collective-permute-start.24 = (bf16[256,1024]{1,0:T(8,128)(2,1)S(1)}, bf16[256,1024]{1,0:T(8,128)(2,1)S(1)}, u32[]{:S(2)}, u32[]{:S(2)}) collective-permute-start(bf16[256,1024]{1,0:T(8,128)(2,1)S(1)} %get-tuple-element.27.batch), channel_id=1, source_target_pairs={{0,8},{8,0},{16,24},{24,16},{1,9},{9,1},{17,25},{25,17},{2,10},{10... | collective-permute-start | bytes 1572872 | tf_op jit(solution)/shard_map/ppermute | solution.py:185
  31.9 7.7 %collective-permute-start.7 = (bf16[256,128]{1,0:T(8,128)(2,1)S(1)}, bf16[256,128]{1,0:T(8,128)(2,1)S(1)}, u32[]{:S(2)}, u32[]{:S(2)}) collective-permute-start(bf16[256,128]{1,0:T(8,128)(2,1)S(1)} %get-tuple-element.22.refs_0_), channel_id=1, source_target_pairs={{0,4},{1,5},{2,6},{3,7},{4,0},{5,1},{6,2},{7,3},{8,12},{9,13},{10,... | collective-permute-start | bytes 196616 | tf_op jit(solution)/shard_map/ppermute | solution.py:185
  33.0 8.6 %collective-permute-start.9 = (bf16[256,128]{1,0:T(8,128)(2,1)S(1)}, bf16[256,128]{1,0:T(8,128)(2,1)S(1)}, u32[]{:S(2)}, u32[]{:S(2)}) collective-permute-start(bf16[256,128]{1,0:T(8,128)(2,1)S(1)} %get-tuple-element.22.refs_0_), channel_id=1, source_target_pairs={{0,6},{1,7},{2,4},{3,5},{4,2},{5,3},{6,0},{7,1},{8,14},{9,15},{10,... | collective-permute-start | bytes 196616 | tf_op jit(solution)/shard_map/ppermute | solution.py:185
  34.4 12.1 %collective-permute-start.11 = (bf16[256,128]{1,0:T(8,128)(2,1)S(1)}, bf16[256,128]{1,0:T(8,128)(2,1)S(1)}, u32[]{:S(2)}, u32[]{:S(2)}) collective-permute-start(bf16[256,128]{1,0:T(8,128)(2,1)S(1)} %get-tuple-element.23.refs_8_), channel_id=1, source_target_pairs={{0,8},{8,0},{16,24},{24,16},{1,9},{9,1},{17,25},{25,17},{2,10},{10... | collective-permute-start | bytes 196616 | tf_op jit(solution)/shard_map/ppermute | solution.py:185
  34.9 11.6 %collective-permute-start.12 = (bf16[256,128]{1,0:T(8,128)(2,1)S(1)}, bf16[256,128]{1,0:T(8,128)(2,1)S(1)}, u32[]{:S(2)}, u32[]{:S(2)}) collective-permute-start(bf16[256,128]{1,0:T(8,128)(2,1)S(1)} %get-tuple-element.23.refs_8_), channel_id=1, source_target_pairs={{0,16},{8,24},{16,0},{24,8},{1,17},{9,25},{17,1},{25,9},{2,18},{10... | collective-permute-start | bytes 196616 | tf_op jit(solution)/shard_map/ppermute | solution.py:185
  39.6 8.6 %collective-permute-start.13 = (bf16[256,128]{1,0:T(8,128)(2,1)S(1)}, bf16[256,128]{1,0:T(8,128)(2,1)S(1)}, u32[]{:S(2)}, u32[]{:S(2)}) collective-permute-start(bf16[256,128]{1,0:T(8,128)(2,1)S(1)} %get-tuple-element.23.refs_8_), channel_id=1, source_target_pairs={{0,24},{8,16},{16,8},{24,0},{1,25},{9,17},{17,9},{25,1},{2,26},{10... | collective-permute-start | bytes 196616 | tf_op jit(solution)/shard_map/ppermute | solution.py:185
  41.6 6.5 %collective-permute-start.6 = (bf16[256,128]{1,0:T(8,128)(2,1)S(1)}, bf16[256,128]{1,0:T(8,128)(2,1)S(1)}, u32[]{:S(2)}, u32[]{:S(2)}) collective-permute-start(bf16[256,128]{1,0:T(8,128)(2,1)S(1)} %collective-permute-done.5.refs_2_), channel_id=1, source_target_pairs={{0,1},{1,0},{2,3},{3,2},{4,5},{5,4},{6,7},{7,6},{8,9},{9,8},{10,11... | collective-permute-start | bytes 196616 | tf_op jit(solution)/shard_map/ppermute | solution.py:185
  48.5 5.2 %collective-permute-start.14 = (bf16[256,128]{1,0:T(8,128)(2,1)S(1)}, bf16[256,128]{1,0:T(8,128)(2,1)S(1)}, u32[]{:S(2)}, u32[]{:S(2)}) collective-permute-start(bf16[256,128]{1,0:T(8,128)(2,1)S(1)} %shard_map.62.refs_0_), channel_id=1, source_target_pairs={{0,2},{1,3},{2,0},{3,1},{4,6},{5,7},{6,4},{7,5},{8,10},{9,11},{10,... | collective-permute-start | bytes 196616 | tf_op jit(solution)/shard_map/ppermute | solution.py:185
  48.8 7.9 %collective-permute-start.15 = (bf16[256,128]{1,0:T(8,128)(2,1)S(1)}, bf16[256,128]{1,0:T(8,128)(2,1)S(1)}, u32[]{:S(2)}, u32[]{:S(2)}) collective-permute-start(bf16[256,128]{1,0:T(8,128)(2,1)S(1)} %shard_map.62.refs_0_), channel_id=1, source_target_pairs={{0,4},{1,5},{2,6},{3,7},{4,0},{5,1},{6,2},{7,3},{8,12},{9,13},{10,... | collective-permute-start | bytes 196616 | tf_op jit(solution)/shard_map/ppermute | solution.py:185
  51.6 6.2 %collective-permute-start.16 = (bf16[256,128]{1,0:T(8,128)(2,1)S(1)}, bf16[256,128]{1,0:T(8,128)(2,1)S(1)}, u32[]{:S(2)}, u32[]{:S(2)}) collective-permute-start(bf16[256,128]{1,0:T(8,128)(2,1)S(1)} %shard_map.62.refs_0_), channel_id=1, source_target_pairs={{0,6},{1,7},{2,4},{3,5},{4,2},{5,3},{6,0},{7,1},{8,14},{9,15},{10,... | collective-permute-start | bytes 196616 | tf_op jit(solution)/shard_map/ppermute | solution.py:185
  57.8 4.8 %collective-permute-start.17 = (bf16[4,256,128]{2,1,0:T(8,128)(2,1)S(1)}, bf16[4,256,128]{2,1,0:T(8,128)(2,1)S(1)}, u32[]{:S(2)}, u32[]{:S(2)}) collective-permute-start(bf16[4,256,128]{2,1,0:T(8,128)(2,1)S(1)} %shard_map.63.half), channel_id=1, source_target_pairs={{0,1},{1,0},{2,3},{3,2},{4,5},{5,4},{6,7},{7,6},{8,9},{9,8},{10,11... | collective-permute-start | bytes 786440 | tf_op jit(solution)/shard_map/ppermute | solution.py:185
  57.9 38.4 %collective-permute-start.25 = (bf16[256,1024]{1,0:T(8,128)(2,1)S(1)}, bf16[256,1024]{1,0:T(8,128)(2,1)S(1)}, u32[]{:S(2)}, u32[]{:S(2)}) collective-permute-start(bf16[256,1024]{1,0:T(8,128)(2,1)S(1)} %get-tuple-element.27.batch), channel_id=1, source_target_pairs={{0,16},{8,24},{16,0},{24,8},{1,17},{9,25},{17,1},{25,9},{2,18},{10... | collective-permute-start | bytes 1572872 | tf_op jit(solution)/shard_map/ppermute | solution.py:185
  59.1 37.2 %collective-permute-start.26 = (bf16[256,1024]{1,0:T(8,128)(2,1)S(1)}, bf16[256,1024]{1,0:T(8,128)(2,1)S(1)}, u32[]{:S(2)}, u32[]{:S(2)}) collective-permute-start(bf16[256,1024]{1,0:T(8,128)(2,1)S(1)} %get-tuple-element.27.batch), channel_id=1, source_target_pairs={{0,24},{8,16},{16,8},{24,0},{1,25},{9,17},{17,9},{25,1},{2,26},{10... | collective-permute-start | bytes 1572872 | tf_op jit(solution)/shard_map/ppermute | solution.py:185
  60.9 19.0 %collective-permute-start.18 = (bf16[4,256,128]{2,1,0:T(8,128)(2,1)S(1)}, bf16[4,256,128]{2,1,0:T(8,128)(2,1)S(1)}, u32[]{:S(2)}, u32[]{:S(2)}) collective-permute-start(bf16[4,256,128]{2,1,0:T(8,128)(2,1)S(1)} %shard_map.63.half), channel_id=1, source_target_pairs={{0,8},{8,0},{16,24},{24,16},{1,9},{9,1},{17,25},{25,17},{2,10},{10... | collective-permute-start | bytes 786440 | tf_op jit(solution)/shard_map/ppermute | solution.py:185
  61.4 33.2 %collective-permute-start.19 = (bf16[4,256,128]{2,1,0:T(8,128)(2,1)S(1)}, bf16[4,256,128]{2,1,0:T(8,128)(2,1)S(1)}, u32[]{:S(2)}, u32[]{:S(2)}) collective-permute-start(bf16[4,256,128]{2,1,0:T(8,128)(2,1)S(1)} %shard_map.63.half), channel_id=1, source_target_pairs={{0,16},{8,24},{16,0},{24,8},{1,17},{9,25},{17,1},{25,9},{2,18},{10... | collective-permute-start | bytes 786440 | tf_op jit(solution)/shard_map/ppermute | solution.py:185
  62.6 32.1 %collective-permute-start.20 = (bf16[4,256,128]{2,1,0:T(8,128)(2,1)S(1)}, bf16[4,256,128]{2,1,0:T(8,128)(2,1)S(1)}, u32[]{:S(2)}, u32[]{:S(2)}) collective-permute-start(bf16[4,256,128]{2,1,0:T(8,128)(2,1)S(1)} %shard_map.63.half), channel_id=1, source_target_pairs={{0,24},{8,16},{16,8},{24,0},{1,25},{9,17},{17,9},{25,1},{2,26},{10... | collective-permute-start | bytes 786440 | tf_op jit(solution)/shard_map/ppermute | solution.py:185
  79.9 16.4 %collective-permute-start.21 = (bf16[4,256,128]{2,1,0:T(8,128)(2,1)S(1)}, bf16[4,256,128]{2,1,0:T(8,128)(2,1)S(1)}, u32[]{:S(2)}, u32[]{:S(2)}) collective-permute-start(bf16[4,256,128]{2,1,0:T(8,128)(2,1)S(1)} %collective-permute-done.18.refs_0_), channel_id=1, source_target_pairs={{0,1},{1,0},{2,3},{3,2},{4,5},{5,4},{6,7},{7,6},{8,9},{9,8},{10,11... | collective-permute-start | bytes 786440 | tf_op jit(solution)/shard_map/ppermute | solution.py:185
  94.7 1.9 %collective-permute-start.23 = (bf16[4,256,128]{2,1,0:T(8,128)(2,1)S(1)}, bf16[4,256,128]{2,1,0:T(8,128)(2,1)S(1)}, u32[]{:S(2)}, u32[]{:S(2)}) collective-permute-start(bf16[4,256,128]{2,1,0:T(8,128)(2,1)S(1)} %collective-permute-done.20.refs_2_), channel_id=1, source_target_pairs={{0,1},{1,0},{2,3},{3,2},{4,5},{5,4},{6,7},{7,6},{8,9},{9,8},{10,11... | collective-permute-start | bytes 786440 | tf_op jit(solution)/shard_map/ppermute | solution.py:185
  (7 other events, 9.2 us)
where the time goes:
time: 101 us
  waiting for transfers between devices  56.7 us (56%)
  starting transfers between devices  28.8 us (29%)
  Pallas kernels  10 us (10%)
  local copies, waits for them, and re-layouts  4.24 us (4%)
    ppermute x27, waiting for transfers between devices, hop(): return lax.ppermute(x, axis, [(k, k ^ m) for k in range(n)])  56.7 us
    ppermute x27, starting transfers between devices, hop(): return lax.ppermute(x, axis, [(k, k ^ m) for k in range(n)])  28.8 us
    pallas_call x7, Pallas kernels, call(): pl.pallas_call(kernel, out_shape=outs[0] if single else outs, in_specs=[p...  10 us
    unnamed x8, local copies, waits for them, and re-layouts  4.24 us
  transfers between devices with their start and end apart: 27, of which 12 were waited for; matrix products, arithmetic and copies ran while one was open for 0% of the time, Pallas kernels for 1%

commit v1 on v0

v1 whole, which is shorter than its diff:
```python
import functools

import jax
import jax.numpy as jnp
from jax import lax
from jax.experimental import pallas as pl
from jax.experimental.pallas import tpu as pltpu
from jax.sharding import PartitionSpec as P


LANE = 128
EXTRA = 16
BF = jnp.bfloat16
F32 = jnp.float32


def mm(left, right, a, b):
    return lax.dot_general(left, right, (((a,), (b,)), ((), ())), preferred_element_type=F32)


def shrink(value, limit):
    return value - jnp.clip(value, -limit, limit)


def expand_keep(sup, width):
    blocks = sup.shape[0]
    row = lax.broadcasted_iota(jnp.int32, (blocks, width), 0)
    col = lax.broadcasted_iota(jnp.int32, (blocks, width), 1)
    spread = jnp.where(col // (width // blocks) == row, 1.0, 0.0).astype(BF)
    return mm(sup.astype(F32).astype(BF), spread, 0, 0).astype(BF)


def split_rows(total):
    hi = total.astype(BF)
    rest = total - hi.astype(F32)
    mid = rest.astype(BF)
    low = (rest - mid.astype(F32)).astype(BF)
    row = lax.broadcasted_iota(jnp.int32, (EXTRA, LANE), 0)
    out = jnp.where(row == 0, hi.astype(F32), 0.0)
    out = jnp.where(row == 1, mid.astype(F32), out)
    return jnp.where(row == 2, low.astype(F32), out)


def block_of(index, size):
    return pl.ds(pl.multiple_of(index * size, size), size)


def prepare(pool_hbm, dic_hbm, sup_hbm, pick_hbm, batch, masked, keep, send, *scratch):
    pool, dic, sup, pick, sems, block_sems = scratch
    v = lax.axis_index("vox")
    frames, width = batch.shape
    blocks = dic.shape[0] // LANE
    copies = [
        pltpu.make_async_copy(source, target, sems.at[i])
        for i, (source, target) in enumerate([(pick_hbm, pick), (sup_hbm, sup), (pool_hbm, pool)])
    ]
    spots = [block_of((v % blocks) ^ r, LANE) for r in range(blocks)]
    parts = [
        pltpu.make_async_copy(dic_hbm.at[at, :], dic.at[at, :], block_sems.at[r])
        for r, at in enumerate(spots)
    ]
    for copy in copies + parts:
        copy.start()
    for copy in copies:
        copy.wait()
    source = lax.broadcasted_iota(jnp.int32, (pool.shape[0], frames), 0)
    chosen = jnp.where(source == pick[...], 1.0, 0.0).astype(BF)
    batch[...] = mm(chosen, pool[...], 0, 0).astype(BF)
    ones = jnp.ones((8, LANE), BF)
    row = lax.broadcasted_iota(jnp.int32, (EXTRA, LANE), 0)
    for i in range(blocks // 2):
        pair = []
        for r in (2 * i, 2 * i + 1):
            parts[r].wait()
            block = dic[spots[r], :] * expand_keep(sup[:, spots[r]], width)
            masked[spots[r], :] = block
            pair.append(block)
        part = mm(batch[...], jnp.concatenate(pair, axis=0), 1, 1)
        keep[i, :frames, :] = part[:, :LANE]
        send[i, :frames, :] = part[:, LANE:].astype(BF)
        for block, out in zip(pair, (keep, send)):
            square = jnp.square(block.astype(F32))
            folded = square[:, :LANE]
            for j in range(1, width // LANE):
                folded = folded + square[:, j * LANE : (j + 1) * LANE]
            hi = folded.astype(BF)
            rest = folded - hi.astype(F32)
            mid = rest.astype(BF)
            low = (rest - mid.astype(F32)).astype(BF)
            energy = (mm(ones, hi, 1, 1) + (mm(ones, mid, 1, 1) + mm(ones, low, 1, 1)))[:1]
            if out is keep:
                out[i, frames:, :] = jnp.where(row == 0, energy, 0.0)
            else:
                out[i, frames:, :] = split_rows(energy).astype(BF)


def gram_part(masked, keep, send):
    v, f = lax.axis_index("vox"), lax.axis_index("frame")
    own = keep.shape[1]
    blocks = masked.shape[0] // LANE
    left = masked[block_of(f, own), :]
    for i in range(blocks // 2):
        pair = [masked[block_of((v % blocks) ^ r, LANE), :] for r in (2 * i, 2 * i + 1)]
        part = mm(left, jnp.concatenate(pair, axis=0), 1, 1)
        keep[i] = part[:, :LANE]
        send[i] = part[:, LANE:].astype(BF)


def pack_sum(total, extra):
    if not extra:
        return total.astype(BF)
    top = total.shape[0] - extra
    energy = jnp.sum(total[top:], axis=0, keepdims=True)
    return jnp.concatenate([total[:top].astype(BF), split_rows(energy).astype(BF)], axis=0)


def fold_core(extra, keep, got, own, *sends):
    own[...] = keep[0] + got[0].astype(F32)
    for i, out in enumerate(sends):
        out[...] = pack_sum(keep[i + 1] + got[i + 1].astype(F32), extra)


def fold_line(own, *rest):
    *gots, first, corr, step = rest
    frames = first.shape[0]
    total = own[...]
    for got in gots:
        total = total + got[...].astype(F32)
    energy = jnp.sum(total[frames:], axis=0, keepdims=True)
    scale = 1.0 / (energy + 1e-05)
    corr[...] = total[:frames]
    first[...] = shrink(total[:frames] * scale, 0.3 * scale).astype(BF)
    step[...] = jnp.broadcast_to(scale, step.shape)


def fold_gram(own, *rest):
    *gots, gram = rest
    total = own[...]
    for got in gots:
        total = total + got[...].astype(F32)
    gram[...] = total.astype(BF)


def second(n_first, n_gram, *refs):
    firsts = refs[:n_first]
    grams = refs[n_first : n_first + n_gram]
    corr, step, codes, square = refs[n_first + n_gram :]
    v, f = lax.axis_index("vox"), lax.axis_index("frame")
    own = grams[0].shape[0]
    for s in range(n_gram):
        square[block_of(f ^ s, own), :] = grams[s][...]
    push = -corr[...]
    for r in range(n_first):
        push = push + mm(firsts[r][...], square[block_of((v % n_first) ^ r, LANE), :], 1, 0)
    scale = step[:1, :]
    codes[...] = shrink(firsts[0][...].astype(F32) - scale * push, 0.3 * scale).astype(BF)


def pack(*refs):
    *parts, out = refs
    for i, part in enumerate(parts):
        out[i] = part[...]


def place(half, other, whole):
    v = lax.axis_index("vox")
    count = half.shape[0]
    for i in range(count):
        whole[:, block_of((v % (2 * count)) ^ (2 * i), LANE)] = half[i]
        whole[:, block_of((v % (2 * count)) ^ (2 * i + 1), LANE)] = other[i]


def own_group(half, other, masked, batch, codes, total):
    f = lax.axis_index("frame")
    place(half, other, codes)
    error = (mm(codes[...], masked[...], 1, 0) - batch[...].astype(F32)).astype(BF)
    rows = total.shape[0]
    total[...] = mm(codes[:, block_of(f, rows)], error, 0, 0)


def add_group(half, other, batch, masked, total, out, codes):
    f = lax.axis_index("frame")
    place(half, other, codes)
    error = (mm(codes[...], masked[...], 1, 0) - batch[...].astype(F32)).astype(BF)
    out[...] = total[...] + mm(codes[:, block_of(f, total.shape[0])], error, 0, 0)


def last_group(scale, half, other, batch, masked, total, sup, out, codes):
    f = lax.axis_index("frame")
    add_group(half, other, batch, masked, total, out, codes)
    kept = expand_keep(sup[:, block_of(f, total.shape[0])], total.shape[1]).astype(F32)
    out[...] = kept * out[...] * scale


def call(kernel, outs, args, scratch=(), flops=0, space=pltpu.VMEM):
    moved = sum(a.size * a.dtype.itemsize for a in (*args, *outs))
    single = len(outs) == 1
    return pl.pallas_call(
        kernel,
        out_shape=outs[0] if single else outs,
        in_specs=[pl.BlockSpec(memory_space=space)] * len(args),
        out_specs=pl.BlockSpec(memory_space=pltpu.VMEM)
        if single
        else [pl.BlockSpec(memory_space=pltpu.VMEM)] * len(outs),
        scratch_shapes=list(scratch),
        compiler_params=pltpu.CompilerParams(vmem_limit_bytes=8 * 2**20),
        cost_estimate=pl.CostEstimate(flops=flops, bytes_accessed=moved, transcendentals=0),
    )(*args)


def shape(dims, dtype):
    return jax.ShapeDtypeStruct(dims, dtype)


def work(pool, dictionary, support, pick):
    n_vox, n_frame = lax.axis_size("vox"), lax.axis_size("frame")
    modes, width = dictionary.shape
    frames = pick.shape[0]
    blocks = modes // LANE
    own = modes // n_frame
    line = [m for m in range(2, blocks, 2)]

    def hop(x, axis, m):
        n = n_vox if axis == "vox" else n_frame
        return lax.ppermute(x, axis, [(k, k ^ m) for k in range(n)])

    def reduce(keep, send, extra):
        tall = keep.shape[1]
        got = hop(send, "vox", 1)
        mine, *sends = call(
            functools.partial(fold_core, extra),
            [shape((tall, LANE), F32)] + [shape((tall, LANE), BF)] * len(line),
            (keep, got),
        )
        gots = [hop(s, "vox", m) for s, m in zip(sends, line)]
        far = blocks
        while far < n_vox:
            total = mine
            for g in gots:
                total = total + g.astype(F32)
            sent = pack_sum(total, extra)
            mine, gots = sent.astype(F32), [hop(sent, "vox", far)]
            far *= 2
        return mine, gots

    sup = support.T
    batch, masked, keep, send = call(
        prepare,
        [
            shape((frames, width), BF),
            shape((modes, width), BF),
            shape((blocks // 2, frames + EXTRA, LANE), F32),
            shape((blocks // 2, frames + EXTRA, LANE), BF),
        ],
        (pool, dictionary, sup, pick.reshape(1, frames)),
        [
            pltpu.VMEM(pool.shape, BF),
            pltpu.VMEM(dictionary.shape, BF),
            pltpu.VMEM(sup.shape, jnp.int32),
            pltpu.VMEM((1, frames), jnp.int32),
            pltpu.SemaphoreType.DMA((3,)),
            pltpu.SemaphoreType.DMA((blocks,)),
        ],
        2 * frames * modes * width,
        pltpu.HBM,
    )
    gram_keep, gram_send = call(
        gram_part,
        [
            shape((blocks // 2, own, LANE), F32),
            shape((blocks // 2, own, LANE), BF),
        ],
        (masked,),
        flops=2 * own * modes * width,
    )
    mine, gots = reduce(keep, send, EXTRA)
    first, corr, step = call(
        fold_line,
        [
            shape((frames, LANE), BF),
            shape((frames, LANE), F32),
            shape((8, LANE), F32),
        ],
        (mine, *gots),
    )
    mine, gots = reduce(gram_keep, gram_send, 0)
    gram = call(fold_gram, [shape((own, LANE), BF)], (mine, *gots))
    firsts = [first] + [hop(first, "vox", m) for m in line]
    grams = [gram] + [hop(gram, "frame", s) for s in range(1, n_frame)]
    odd = [hop(first, "vox", 1)] + [hop(x, "vox", 1) for x in firsts[1:]]
    ordered = [x for pair in zip(firsts, odd) for x in pair]
    code = call(
        functools.partial(second, blocks, n_frame),
        [shape((frames, LANE), BF)],
        (*ordered, *grams, corr, step),
        [pltpu.VMEM((modes, LANE), BF)],
        2 * frames * modes * LANE,
    )
    half = call(
        pack, [shape((blocks // 2, frames, LANE), BF)], (code, *[hop(code, "vox", m) for m in line])
    )
    groups = range(1, n_frame)
    batches = [hop(batch, "frame", s) for s in groups]
    halves = [hop(half, "frame", s) for s in groups]
    other = hop(half, "vox", 1)
    others = [hop(h, "vox", 1) for h in halves]
    codes, total = call(
        own_group,
        [shape((frames, modes), BF), shape((own, width), F32)],
        (half, other, masked, batch),
        flops=2 * frames * modes * width,
    )
    held = [pltpu.VMEM((frames, modes), BF)]
    work_size = 2 * frames * (modes + own) * width
    for i in range(n_frame - 1):
        args = (halves[i], others[i], batches[i], masked, total)
        if i < n_frame - 2:
            total = call(add_group, [shape((own, width), F32)], args, held, work_size)
        else:
            total = call(
                functools.partial(last_group, 1.0 / (frames * n_frame)),
                [shape((own, width), F32)],
                (*args, sup),
                held,
                work_size,
            )
    return codes, total


def solution(mesh):
    placed = (P("frame", "vox"), P(None, "vox"), P(None, "vox"), P("frame"))
    return jax.shard_map(
        work,
        mesh=mesh,
        in_specs=placed,
        out_specs=(P("frame", None), P("frame", "vox")),
        check_vma=False,
    )
```

time: 101 us -> 96.7 us (0.957)
  waiting for transfers between devices: 56.7 us -> 47.3 us
  starting transfers between devices: 28.8 us -> 32.9 us
  Pallas kernels: 10 us -> 11.2 us
    ppermute x27 -> x31, waiting for transfers between devices: 56.7 us -> 47.3 us  [hop(): return lax.ppermute(x, axis, [(k, k ^ m) for k in range(n)])]
    ppermute x27 -> x31, starting transfers between devices: 28.8 us -> 32.9 us  [hop(): return lax.ppermute(x, axis, [(k, k ^ m) for k in range(n)])]
    pallas_call x7 -> x12, Pallas kernels: 10 us -> 11.2 us  [call(): pl.pallas_call(kernel, out_shape=outs[0] if single else outs, in_specs=[p...]
    unnamed x8 -> x10, local copies, waits for them, and re-layouts: 4.24 us -> 4.25 us
  transfers between devices with their start and end apart: 27 -> 31, of which waited for: 12 -> 12; matrix products, arithmetic and copies ran while one was open for 0% -> 0% of each run, Pallas kernels for 1% -> 5%
where the time goes in v1:
time: 96.7 us; the launch traced here: 96.5 us
  waiting for transfers between devices  47.3 us (49%)
  starting transfers between devices  32.9 us (34%)
  Pallas kernels  11.2 us (12%)
  local copies, waits for them, and re-layouts  4.25 us (4%)
    ppermute x31, waiting for transfers between devices, hop(): return lax.ppermute(x, axis, [(k, k ^ m) for k in range(n)])  47.3 us
    ppermute x31, starting transfers between devices, hop(): return lax.ppermute(x, axis, [(k, k ^ m) for k in range(n)])  32.9 us
    pallas_call x12, Pallas kernels, call(): pl.pallas_call(kernel, out_shape=outs[0] if single else outs, in_specs=[p...  11.2 us
    unnamed x10, local copies, waits for them, and re-layouts  4.25 us
  transfers between devices with their start and end apart: 31, of which 12 were waited for; matrix products, arithmetic and copies ran while one was open for 0% of the time, Pallas kernels for 5%

profile of v1, /device:TPU:0, one launch (start us, length us, event | category | flops | bytes accessed | tf_op | source)
XLA Modules:
  0.0 96.5 jit_solution(5693228645005896038)
XLA Ops:
  0.6 1.6 %copy-done = bf16[1024,1024]{1,0:T(8,128)(2,1)S(1)} copy-done((bf16[1024,1024]{1,0:T(8,128)(2,1)S(1)}, bf16[1024,1024]{1,0:T(8,128)(2,1)}, u32[]{:S(2)}) %copy-start) | copy-done | bytes 2097176
  2.2 1.2 %copy-done.1 = bf16[512,1024]{1,0:T(8,128)(2,1)S(1)} copy-done((bf16[512,1024]{1,0:T(8,128)(2,1)S(1)}, bf16[512,1024]{1,0:T(8,128)(2,1)}, u32[]{:S(2)}) %copy-start.1) | copy-done | bytes 1048600
  4.9 4.6 %shard_map.59 = (bf16[256,1024]{1,0:T(8,128)(2,1)S(1)}, bf16[1024,1024]{1,0:T(8,128)(2,1)S(1)}, f32[4,272,128]{2,1,0:T(8,128)S(1)}, bf16[4,272,128]{2,1,0:T(8,128)(2,1)S(1)}) custom-call(bf16[512,1024]{1,0:T(8,128)(2,1)S(1)} %copy-done.1, bf16[1024,1024]{1,0:T(8,128)(2,1)S(1)} %copy-done, s32[8,1024]{1,0:T(8,128)S(1)} %bitcast.2, s32[1,256]{1,0:T(1,128)S(1)} %bitcast.4), custom_call_target="tpu_custom_call" | custom-call | flops 536870912 | bytes 6636544 | tf_op jit(solution)/shard_map/pallas_call | solution.py:198
  10.9 1.5 %collective-permute-done.11.got = bf16[4,256,128]{2,1,0:T(8,128)(2,1)S(1)} collective-permute-done((bf16[4,256,128]{2,1,0:T(8,128)(2,1)S(1)}, bf16[4,256,128]{2,1,0:T(8,128)(2,1)S(1)}, u32[]{:S(2)}, u32[]{:S(2)}) %collective-permute-start.11) | collective-permute-done | bytes 262176 | tf_op jit(solution)/shard_map/ppermute | solution.py:225
  12.4 2.8 %collective-permute-start.12 = (bf16[256,128]{1,0:T(8,128)(2,1)S(1)}, bf16[256,128]{1,0:T(8,128)(2,1)S(1)}, u32[]{:S(2)}, u32[]{:S(2)}) collective-permute-start(bf16[256,128]{1,0:T(8,128)(2,1)S(1)} %get-tuple-element.32), channel_id=1, source_target_pairs={{0,2},{1,3},{2,0},{3,1},{4,6},{5,7},{6,4},{7,5},{8,10},{9,11},{10,... | collective-permute-start | bytes 196616 | tf_op jit(solution)/shard_map/ppermute | solution.py:225
  15.2 2.6 %collective-permute-start.13 = (bf16[256,128]{1,0:T(8,128)(2,1)S(1)}, bf16[256,128]{1,0:T(8,128)(2,1)S(1)}, u32[]{:S(2)}, u32[]{:S(2)}) collective-permute-start(bf16[256,128]{1,0:T(8,128)(2,1)S(1)} %get-tuple-element.33), channel_id=1, source_target_pairs={{0,4},{1,5},{2,6},{3,7},{4,0},{5,1},{6,2},{7,3},{8,12},{9,13},{10,... | collective-permute-start | bytes 196616 | tf_op jit(solution)/shard_map/ppermute | solution.py:225
  18.8 3.5 %collective-permute-start.2 = (bf16[272,128]{1,0:T(8,128)(2,1)S(1)}, bf16[272,128]{1,0:T(8,128)(2,1)S(1)}, u32[]{:S(2)}, u32[]{:S(2)}) collective-permute-start(bf16[272,128]{1,0:T(8,128)(2,1)S(1)} %get-tuple-element.25), channel_id=1, source_target_pairs={{0,4},{1,5},{2,6},{3,7},{4,0},{5,1},{6,2},{7,3},{8,12},{9,13},{10,... | collective-permute-start | bytes 208904 | tf_op jit(solution)/shard_map/ppermute | solution.py:225
  22.9 1.7 %collective-permute-done.14.rest_2_ = bf16[256,128]{1,0:T(8,128)(2,1)S(1)} collective-permute-done((bf16[256,128]{1,0:T(8,128)(2,1)S(1)}, bf16[256,128]{1,0:T(8,128)(2,1)S(1)}, u32[]{:S(2)}, u32[]{:S(2)}) %collective-permute-start.14) | collective-permute-done | bytes 65568 | tf_op jit(solution)/shard_map/ppermute | solution.py:225
  24.6 1.5 %collective-permute-start.15 = (bf16[256,128]{1,0:T(8,128)(2,1)S(1)}, bf16[256,128]{1,0:T(8,128)(2,1)S(1)}, u32[]{:S(2)}, u32[]{:S(2)}) collective-permute-start(bf16[256,128]{1,0:T(8,128)(2,1)S(1)} %shard_map.64.refs_8_), channel_id=1, source_target_pairs={{0,8},{8,0},{16,24},{24,16},{1,9},{9,1},{17,25},{25,17},{2,10},{10... | collective-permute-start | bytes 196616 | tf_op jit(solution)/shard_map/ppermute | solution.py:225
  26.1 1.5 %collective-permute-start.16 = (bf16[256,128]{1,0:T(8,128)(2,1)S(1)}, bf16[256,128]{1,0:T(8,128)(2,1)S(1)}, u32[]{:S(2)}, u32[]{:S(2)}) collective-permute-start(bf16[256,128]{1,0:T(8,128)(2,1)S(1)} %shard_map.64.refs_8_), channel_id=1, source_target_pairs={{0,16},{8,24},{16,0},{24,8},{1,17},{9,25},{17,1},{25,9},{2,18},{10... | collective-permute-start | bytes 196616 | tf_op jit(solution)/shard_map/ppermute | solution.py:225
  28.2 1.2 %collective-permute-done.2.rest_1_ = bf16[272,128]{1,0:T(8,128)(2,1)S(1)} collective-permute-done((bf16[272,128]{1,0:T(8,128)(2,1)S(1)}, bf16[272,128]{1,0:T(8,128)(2,1)S(1)}, u32[]{:S(2)}, u32[]{:S(2)}) %collective-permute-start.2) | collective-permute-done | bytes 69664 | tf_op jit(solution)/shard_map/ppermute | solution.py:225
  29.4 2.4 %collective-permute-start.17 = (bf16[256,128]{1,0:T(8,128)(2,1)S(1)}, bf16[256,128]{1,0:T(8,128)(2,1)S(1)}, u32[]{:S(2)}, u32[]{:S(2)}) collective-permute-start(bf16[256,128]{1,0:T(8,128)(2,1)S(1)} %shard_map.64.refs_8_), channel_id=1, source_target_pairs={{0,24},{8,16},{16,8},{24,0},{1,25},{9,17},{17,9},{25,1},{2,26},{10... | collective-permute-start | bytes 196616 | tf_op jit(solution)/shard_map/ppermute | solution.py:225
  31.9 2.7 %collective-permute-start.9 = (bf16[256,128]{1,0:T(8,128)(2,1)S(1)}, bf16[256,128]{1,0:T(8,128)(2,1)S(1)}, u32[]{:S(2)}, u32[]{:S(2)}) collective-permute-start(bf16[256,128]{1,0:T(8,128)(2,1)S(1)} %get-tuple-element.27.refs_0_), channel_id=1, source_target_pairs={{0,6},{1,7},{2,4},{3,5},{4,2},{5,3},{6,0},{7,1},{8,14},{9,15},{10,... | collective-permute-start | bytes 196616 | tf_op jit(solution)/shard_map/ppermute | solution.py:225
  36.4 4.7 %collective-permute-done.17.refs_11_ = bf16[256,128]{1,0:T(8,128)(2,1)S(1)} collective-permute-done((bf16[256,128]{1,0:T(8,128)(2,1)S(1)}, bf16[256,128]{1,0:T(8,128)(2,1)S(1)}, u32[]{:S(2)}, u32[]{:S(2)}) %collective-permute-start.17) | collective-permute-done | bytes 65568 | tf_op jit(solution)/shard_map/ppermute | solution.py:225
  43.4 1.5 %collective-permute-start.18 = (bf16[256,128]{1,0:T(8,128)(2,1)S(1)}, bf16[256,128]{1,0:T(8,128)(2,1)S(1)}, u32[]{:S(2)}, u32[]{:S(2)}) collective-permute-start(bf16[256,128]{1,0:T(8,128)(2,1)S(1)} %shard_map.65.refs_0_), channel_id=1, source_target_pairs={{0,2},{1,3},{2,0},{3,1},{4,6},{5,7},{6,4},{7,5},{8,10},{9,11},{10,... | collective-permute-start | bytes 196616 | tf_op jit(solution)/shard_map/ppermute | solution.py:225
  44.8 1.4 %collective-permute-start.19 = (bf16[256,128]{1,0:T(8,128)(2,1)S(1)}, bf16[256,128]{1,0:T(8,128)(2,1)S(1)}, u32[]{:S(2)}, u32[]{:S(2)}) collective-permute-start(bf16[256,128]{1,0:T(8,128)(2,1)S(1)} %shard_map.65.refs_0_), channel_id=1, source_target_pairs={{0,4},{1,5},{2,6},{3,7},{4,0},{5,1},{6,2},{7,3},{8,12},{9,13},{10,... | collective-permute-start | bytes 196616 | tf_op jit(solution)/shard_map/ppermute | solution.py:225
  46.2 1.6 %collective-permute-start.20 = (bf16[256,128]{1,0:T(8,128)(2,1)S(1)}, bf16[256,128]{1,0:T(8,128)(2,1)S(1)}, u32[]{:S(2)}, u32[]{:S(2)}) collective-permute-start(bf16[256,128]{1,0:T(8,128)(2,1)S(1)} %shard_map.65.refs_0_), channel_id=1, source_target_pairs={{0,6},{1,7},{2,4},{3,5},{4,2},{5,3},{6,0},{7,1},{8,14},{9,15},{10,... | collective-permute-start | bytes 196616 | tf_op jit(solution)/shard_map/ppermute | solution.py:225
  47.8 5.3 %collective-permute-done.19.refs_2_ = bf16[256,128]{1,0:T(8,128)(2,1)S(1)} collective-permute-done((bf16[256,128]{1,0:T(8,128)(2,1)S(1)}, bf16[256,128]{1,0:T(8,128)(2,1)S(1)}, u32[]{:S(2)}, u32[]{:S(2)}) %collective-permute-start.19) | collective-permute-done | bytes 65568 | tf_op jit(solution)/shard_map/ppermute | solution.py:225
  54.1 1.3 %collective-permute-start.27 = (bf16[256,1024]{1,0:T(8,128)(2,1)S(1)}, bf16[256,1024]{1,0:T(8,128)(2,1)S(1)}, u32[]{:S(2)}, u32[]{:S(2)}) collective-permute-start(bf16[256,1024]{1,0:T(8,128)(2,1)S(1)} %get-tuple-element.37.batch), channel_id=1, source_target_pairs={{0,16},{8,24},{16,0},{24,8},{1,17},{9,25},{17,1},{25,9},{2,18},{10... | collective-permute-start | bytes 1572872 | tf_op jit(solution)/shard_map/ppermute | solution.py:225
  56.1 2.2 %collective-permute-start.24 = (bf16[256,1024]{1,0:T(8,128)(2,1)S(1)}, bf16[256,1024]{1,0:T(8,128)(2,1)S(1)}, u32[]{:S(2)}, u32[]{:S(2)}) collective-permute-start(bf16[256,1024]{1,0:T(8,128)(2,1)S(1)} %get-tuple-element.37.batch), channel_id=1, source_target_pairs={{0,24},{8,16},{16,8},{24,0},{1,25},{9,17},{17,9},{25,1},{2,26},{10... | collective-permute-start | bytes 1572872 | tf_op jit(solution)/shard_map/ppermute | solution.py:225
  59.0 3.5 %collective-permute-done.28.half = bf16[4,256,128]{2,1,0:T(8,128)(2,1)S(1)} collective-permute-done((bf16[4,256,128]{2,1,0:T(8,128)(2,1)S(1)}, bf16[4,256,128]{2,1,0:T(8,128)(2,1)S(1)}, u32[]{:S(2)}, u32[]{:S(2)}) %collective-permute-start.28) | collective-permute-done | bytes 262176 | tf_op jit(solution)/shard_map/ppermute | solution.py:225
  62.5 28.0 %collective-permute-done.25.half = bf16[4,256,128]{2,1,0:T(8,128)(2,1)S(1)} collective-permute-done((bf16[4,256,128]{2,1,0:T(8,128)(2,1)S(1)}, bf16[4,256,128]{2,1,0:T(8,128)(2,1)S(1)}, u32[]{:S(2)}, u32[]{:S(2)}) %collective-permute-start.25) | collective-permute-done | bytes 262176 | tf_op jit(solution)/shard_map/ppermute | solution.py:225
  92.1 1.1 %shard_map.68.total = f32[256,1024]{1,0:T(8,128)S(1)} custom-call(bf16[4,256,128]{2,1,0:T(8,128)(2,1)S(1)} %collective-permute-done.28.half, bf16[4,256,128]{2,1,0:T(8,128)(2,1)S(1)} %collective-permute-done.29.other, bf16[256,1024]{1,0:T(8,128)(2,1)S(1)} %collective-permute-done.30.batch, bf16[1024,1024]{1,0:T(8,128)(2,1)S(1)} %get-tuple-element.28.masked, ...), custom_call_target="tpu_custom_call" | custom-call | flops 671088640 | bytes 5242880 | tf_op jit(solution)/shard_map/pallas_call | solution.py:198
  94.3 2.2 %shard_map.70 = f32[256,1024]{1,0:T(8,128)} custom-call(bf16[4,256,128]{2,1,0:T(8,128)(2,1)S(1)} %collective-permute-done.22.half, bf16[4,256,128]{2,1,0:T(8,128)(2,1)S(1)} %collective-permute-done.23.other, bf16[256,1024]{1,0:T(8,128)(2,1)S(1)} %collective-permute-done.24.batch, bf16[1024,1024]{1,0:T(8,128)(2,1)S(1)} %get-tuple-element.28.masked, ...), custom_call_target="tpu_custom_call" | custom-call | flops 671088640 | bytes 5275648 | tf_op jit(solution)/shard_map/pallas_call | solution.py:198
  (60 shorter events, 14.0 us)
Async XLA Ops:
  9.5 8.3 %collective-permute-start = (bf16[4,272,128]{2,1,0:T(8,128)(2,1)S(1)}, bf16[4,272,128]{2,1,0:T(8,128)(2,1)S(1)}, u32[]{:S(2)}, u32[]{:S(2)}) collective-permute-start(bf16[4,272,128]{2,1,0:T(8,128)(2,1)S(1)} %get-tuple-element.22), channel_id=1, source_target_pairs={{0,1},{1,0},{2,3},{3,2},{4,5},{5,4},{6,7},{7,6},{8,9},{9,8},{10,11... | collective-permute-start | bytes 835592 | tf_op jit(solution)/shard_map/ppermute | solution.py:225
  12.4 9.9 %collective-permute-start.12 = (bf16[256,128]{1,0:T(8,128)(2,1)S(1)}, bf16[256,128]{1,0:T(8,128)(2,1)S(1)}, u32[]{:S(2)}, u32[]{:S(2)}) collective-permute-start(bf16[256,128]{1,0:T(8,128)(2,1)S(1)} %get-tuple-element.32), channel_id=1, source_target_pairs={{0,2},{1,3},{2,0},{3,1},{4,6},{5,7},{6,4},{7,5},{8,10},{9,11},{10,... | collective-permute-start | bytes 196616 | tf_op jit(solution)/shard_map/ppermute | solution.py:225
  15.2 7.7 %collective-permute-start.13 = (bf16[256,128]{1,0:T(8,128)(2,1)S(1)}, bf16[256,128]{1,0:T(8,128)(2,1)S(1)}, u32[]{:S(2)}, u32[]{:S(2)}) collective-permute-start(bf16[256,128]{1,0:T(8,128)(2,1)S(1)} %get-tuple-element.33), channel_id=1, source_target_pairs={{0,4},{1,5},{2,6},{3,7},{4,0},{5,1},{6,2},{7,3},{8,12},{9,13},{10,... | collective-permute-start | bytes 196616 | tf_op jit(solution)/shard_map/ppermute | solution.py:225
  17.8 6.8 %collective-permute-start.14 = (bf16[256,128]{1,0:T(8,128)(2,1)S(1)}, bf16[256,128]{1,0:T(8,128)(2,1)S(1)}, u32[]{:S(2)}, u32[]{:S(2)}) collective-permute-start(bf16[256,128]{1,0:T(8,128)(2,1)S(1)} %get-tuple-element.34), channel_id=1, source_target_pairs={{0,6},{1,7},{2,4},{3,5},{4,2},{5,3},{6,0},{7,1},{8,14},{9,15},{10,... | collective-permute-start | bytes 196616 | tf_op jit(solution)/shard_map/ppermute | solution.py:225
  17.9 9.8 %collective-permute-start.1 = (bf16[272,128]{1,0:T(8,128)(2,1)S(1)}, bf16[272,128]{1,0:T(8,128)(2,1)S(1)}, u32[]{:S(2)}, u32[]{:S(2)}) collective-permute-start(bf16[272,128]{1,0:T(8,128)(2,1)S(1)} %get-tuple-element.24), channel_id=1, source_target_pairs={{0,2},{1,3},{2,0},{3,1},{4,6},{5,7},{6,4},{7,5},{8,10},{9,11},{10,... | collective-permute-start | bytes 208904 | tf_op jit(solution)/shard_map/ppermute | solution.py:225
  18.8 10.6 %collective-permute-start.2 = (bf16[272,128]{1,0:T(8,128)(2,1)S(1)}, bf16[272,128]{1,0:T(8,128)(2,1)S(1)}, u32[]{:S(2)}, u32[]{:S(2)}) collective-permute-start(bf16[272,128]{1,0:T(8,128)(2,1)S(1)} %get-tuple-element.25), channel_id=1, source_target_pairs={{0,4},{1,5},{2,6},{3,7},{4,0},{5,1},{6,2},{7,3},{8,12},{9,13},{10,... | collective-permute-start | bytes 208904 | tf_op jit(solution)/shard_map/ppermute | solution.py:225
  22.3 9.5 %collective-permute-start.3 = (bf16[272,128]{1,0:T(8,128)(2,1)S(1)}, bf16[272,128]{1,0:T(8,128)(2,1)S(1)}, u32[]{:S(2)}, u32[]{:S(2)}) collective-permute-start(bf16[272,128]{1,0:T(8,128)(2,1)S(1)} %get-tuple-element.26), channel_id=1, source_target_pairs={{0,6},{1,7},{2,4},{3,5},{4,2},{5,3},{6,0},{7,1},{8,14},{9,15},{10,... | collective-permute-start | bytes 208904 | tf_op jit(solution)/shard_map/ppermute | solution.py:225
  24.6 10.1 %collective-permute-start.15 = (bf16[256,128]{1,0:T(8,128)(2,1)S(1)}, bf16[256,128]{1,0:T(8,128)(2,1)S(1)}, u32[]{:S(2)}, u32[]{:S(2)}) collective-permute-start(bf16[256,128]{1,0:T(8,128)(2,1)S(1)} %shard_map.64.refs_8_), channel_id=1, source_target_pairs={{0,8},{8,0},{16,24},{24,16},{1,9},{9,1},{17,25},{25,17},{2,10},{10... | collective-permute-start | bytes 196616 | tf_op jit(solution)/shard_map/ppermute | solution.py:225
  26.1 9.5 %collective-permute-start.16 = (bf16[256,128]{1,0:T(8,128)(2,1)S(1)}, bf16[256,128]{1,0:T(8,128)(2,1)S(1)}, u32[]{:S(2)}, u32[]{:S(2)}) collective-permute-start(bf16[256,128]{1,0:T(8,128)(2,1)S(1)} %shard_map.64.refs_8_), channel_id=1, source_target_pairs={{0,16},{8,24},{16,0},{24,8},{1,17},{9,25},{17,1},{25,9},{2,18},{10... | collective-permute-start | bytes 196616 | tf_op jit(solution)/shard_map/ppermute | solution.py:225
  27.7 28.4 %collective-permute-start.30 = (bf16[256,1024]{1,0:T(8,128)(2,1)S(1)}, bf16[256,1024]{1,0:T(8,128)(2,1)S(1)}, u32[]{:S(2)}, u32[]{:S(2)}) collective-permute-start(bf16[256,1024]{1,0:T(8,128)(2,1)S(1)} %get-tuple-element.37.batch), channel_id=1, source_target_pairs={{0,8},{8,0},{16,24},{24,16},{1,9},{9,1},{17,25},{25,17},{2,10},{10... | collective-permute-start | bytes 1572872 | tf_op jit(solution)/shard_map/ppermute | solution.py:225
  29.4 11.7 %collective-permute-start.17 = (bf16[256,128]{1,0:T(8,128)(2,1)S(1)}, bf16[256,128]{1,0:T(8,128)(2,1)S(1)}, u32[]{:S(2)}, u32[]{:S(2)}) collective-permute-start(bf16[256,128]{1,0:T(8,128)(2,1)S(1)} %shard_map.64.refs_8_), channel_id=1, source_target_pairs={{0,24},{8,16},{16,8},{24,0},{1,25},{9,17},{17,9},{25,1},{2,26},{10... | collective-permute-start | bytes 196616 | tf_op jit(solution)/shard_map/ppermute | solution.py:225
  31.9 9.2 %collective-permute-start.9 = (bf16[256,128]{1,0:T(8,128)(2,1)S(1)}, bf16[256,128]{1,0:T(8,128)(2,1)S(1)}, u32[]{:S(2)}, u32[]{:S(2)}) collective-permute-start(bf16[256,128]{1,0:T(8,128)(2,1)S(1)} %get-tuple-element.27.refs_0_), channel_id=1, source_target_pairs={{0,6},{1,7},{2,4},{3,5},{4,2},{5,3},{6,0},{7,1},{8,14},{9,15},{10,... | collective-permute-start | bytes 196616 | tf_op jit(solution)/shard_map/ppermute | solution.py:225
  34.7 6.9 %collective-permute-start.5 = (bf16[256,128]{1,0:T(8,128)(2,1)S(1)}, bf16[256,128]{1,0:T(8,128)(2,1)S(1)}, u32[]{:S(2)}, u32[]{:S(2)}) collective-permute-start(bf16[256,128]{1,0:T(8,128)(2,1)S(1)} %get-tuple-element.27.refs_0_), channel_id=1, source_target_pairs={{0,2},{1,3},{2,0},{3,1},{4,6},{5,7},{6,4},{7,5},{8,10},{9,11},{10,... | collective-permute-start | bytes 196616 | tf_op jit(solution)/shard_map/ppermute | solution.py:225
  35.6 6.1 %collective-permute-start.7 = (bf16[256,128]{1,0:T(8,128)(2,1)S(1)}, bf16[256,128]{1,0:T(8,128)(2,1)S(1)}, u32[]{:S(2)}, u32[]{:S(2)}) collective-permute-start(bf16[256,128]{1,0:T(8,128)(2,1)S(1)} %get-tuple-element.27.refs_0_), channel_id=1, source_target_pairs={{0,4},{1,5},{2,6},{3,7},{4,0},{5,1},{6,2},{7,3},{8,12},{9,13},{10,... | collective-permute-start | bytes 196616 | tf_op jit(solution)/shard_map/ppermute | solution.py:225
  43.4 4.5 %collective-permute-start.18 = (bf16[256,128]{1,0:T(8,128)(2,1)S(1)}, bf16[256,128]{1,0:T(8,128)(2,1)S(1)}, u32[]{:S(2)}, u32[]{:S(2)}) collective-permute-start(bf16[256,128]{1,0:T(8,128)(2,1)S(1)} %shard_map.65.refs_0_), channel_id=1, source_target_pairs={{0,2},{1,3},{2,0},{3,1},{4,6},{5,7},{6,4},{7,5},{8,10},{9,11},{10,... | collective-permute-start | bytes 196616 | tf_op jit(solution)/shard_map/ppermute | solution.py:225
  44.8 8.3 %collective-permute-start.19 = (bf16[256,128]{1,0:T(8,128)(2,1)S(1)}, bf16[256,128]{1,0:T(8,128)(2,1)S(1)}, u32[]{:S(2)}, u32[]{:S(2)}) collective-permute-start(bf16[256,128]{1,0:T(8,128)(2,1)S(1)} %shard_map.65.refs_0_), channel_id=1, source_target_pairs={{0,4},{1,5},{2,6},{3,7},{4,0},{5,1},{6,2},{7,3},{8,12},{9,13},{10,... | collective-permute-start | bytes 196616 | tf_op jit(solution)/shard_map/ppermute | solution.py:225
  46.2 7.0 %collective-permute-start.20 = (bf16[256,128]{1,0:T(8,128)(2,1)S(1)}, bf16[256,128]{1,0:T(8,128)(2,1)S(1)}, u32[]{:S(2)}, u32[]{:S(2)}) collective-permute-start(bf16[256,128]{1,0:T(8,128)(2,1)S(1)} %shard_map.65.refs_0_), channel_id=1, source_target_pairs={{0,6},{1,7},{2,4},{3,5},{4,2},{5,3},{6,0},{7,1},{8,14},{9,15},{10,... | collective-permute-start | bytes 196616 | tf_op jit(solution)/shard_map/ppermute | solution.py:225
  53.2 5.2 %collective-permute-start.21 = (bf16[4,256,128]{2,1,0:T(8,128)(2,1)S(1)}, bf16[4,256,128]{2,1,0:T(8,128)(2,1)S(1)}, u32[]{:S(2)}, u32[]{:S(2)}) collective-permute-start(bf16[4,256,128]{2,1,0:T(8,128)(2,1)S(1)} %shard_map.66.half), channel_id=1, source_target_pairs={{0,1},{1,0},{2,3},{3,2},{4,5},{5,4},{6,7},{7,6},{8,9},{9,8},{10,11... | collective-permute-start | bytes 786440 | tf_op jit(solution)/shard_map/ppermute | solution.py:225
  53.3 9.2 %collective-permute-start.28 = (bf16[4,256,128]{2,1,0:T(8,128)(2,1)S(1)}, bf16[4,256,128]{2,1,0:T(8,128)(2,1)S(1)}, u32[]{:S(2)}, u32[]{:S(2)}) collective-permute-start(bf16[4,256,128]{2,1,0:T(8,128)(2,1)S(1)} %shard_map.66.half), channel_id=1, source_target_pairs={{0,8},{8,0},{16,24},{24,16},{1,9},{9,1},{17,25},{25,17},{2,10},{10... | collective-permute-start | bytes 786440 | tf_op jit(solution)/shard_map/ppermute | solution.py:225
  54.1 39.1 %collective-permute-start.27 = (bf16[256,1024]{1,0:T(8,128)(2,1)S(1)}, bf16[256,1024]{1,0:T(8,128)(2,1)S(1)}, u32[]{:S(2)}, u32[]{:S(2)}) collective-permute-start(bf16[256,1024]{1,0:T(8,128)(2,1)S(1)} %get-tuple-element.37.batch), channel_id=1, source_target_pairs={{0,16},{8,24},{16,0},{24,8},{1,17},{9,25},{17,1},{25,9},{2,18},{10... | collective-permute-start | bytes 1572872 | tf_op jit(solution)/shard_map/ppermute | solution.py:225
  55.4 35.1 %collective-permute-start.25 = (bf16[4,256,128]{2,1,0:T(8,128)(2,1)S(1)}, bf16[4,256,128]{2,1,0:T(8,128)(2,1)S(1)}, u32[]{:S(2)}, u32[]{:S(2)}) collective-permute-start(bf16[4,256,128]{2,1,0:T(8,128)(2,1)S(1)} %shard_map.66.half), channel_id=1, source_target_pairs={{0,16},{8,24},{16,0},{24,8},{1,17},{9,25},{17,1},{25,9},{2,18},{10... | collective-permute-start | bytes 786440 | tf_op jit(solution)/shard_map/ppermute | solution.py:225
  56.1 38.2 %collective-permute-start.24 = (bf16[256,1024]{1,0:T(8,128)(2,1)S(1)}, bf16[256,1024]{1,0:T(8,128)(2,1)S(1)}, u32[]{:S(2)}, u32[]{:S(2)}) collective-permute-start(bf16[256,1024]{1,0:T(8,128)(2,1)S(1)} %get-tuple-element.37.batch), channel_id=1, source_target_pairs={{0,24},{8,16},{16,8},{24,0},{1,25},{9,17},{17,9},{25,1},{2,26},{10... | collective-permute-start | bytes 1572872 | tf_op jit(solution)/shard_map/ppermute | solution.py:225
  58.3 32.2 %collective-permute-start.22 = (bf16[4,256,128]{2,1,0:T(8,128)(2,1)S(1)}, bf16[4,256,128]{2,1,0:T(8,128)(2,1)S(1)}, u32[]{:S(2)}, u32[]{:S(2)}) collective-permute-start(bf16[4,256,128]{2,1,0:T(8,128)(2,1)S(1)} %shard_map.66.half), channel_id=1, source_target_pairs={{0,24},{8,16},{16,8},{24,0},{1,25},{9,17},{17,9},{25,1},{2,26},{10... | collective-permute-start | bytes 786440 | tf_op jit(solution)/shard_map/ppermute | solution.py:225
  62.5 29.6 %collective-permute-start.29 = (bf16[4,256,128]{2,1,0:T(8,128)(2,1)S(1)}, bf16[4,256,128]{2,1,0:T(8,128)(2,1)S(1)}, u32[]{:S(2)}, u32[]{:S(2)}) collective-permute-start(bf16[4,256,128]{2,1,0:T(8,128)(2,1)S(1)} %collective-permute-done.28.half), channel_id=1, source_target_pairs={{0,1},{1,0},{2,3},{3,2},{4,5},{5,4},{6,7},{7,6},{8,9},{9,8},{10,11... | collective-permute-start | bytes 786440 | tf_op jit(solution)/shard_map/ppermute | solution.py:225
  (12 other events, 18.7 us)

commit v2 on v1

--- a/solution.py
+++ b/solution.py
@@ -45,53 +45,58 @@
     return pl.ds(pl.multiple_of(index * size, size), size)
 
 
-def prepare(pool_hbm, dic_hbm, sup_hbm, pick_hbm, batch, masked, keep, send, *scratch):
-    pool, dic, sup, pick, sems, block_sems = scratch
+def load(pool_hbm, dic_hbm, sup_hbm, pick_hbm, batch, dic, sup, pool, pick, sems):
+    frames = batch.shape[0]
+    pairs = [(pick_hbm, pick), (pool_hbm, pool), (sup_hbm, sup), (dic_hbm, dic)]
+    copies = [pltpu.make_async_copy(a, b, sems.at[i]) for i, (a, b) in enumerate(pairs)]
+    for copy in copies:
+        copy.start()
+    copies[0].wait()
+    source = lax.broadcasted_iota(jnp.int32, (pool.shape[0], frames), 0)
+    chosen = jnp.where(source == pick[...], 1.0, 0.0).astype(BF)
+    copies[1].wait()
+    batch[...] = mm(chosen, pool[...], 0, 0).astype(BF)
+    copies[2].wait()
+    copies[3].wait()
+
+
+def blocks_of(odd, dic, sup, batch, masked, out):
     v = lax.axis_index("vox")
     frames, width = batch.shape
     blocks = dic.shape[0] // LANE
-    copies = [
-        pltpu.make_async_copy(source, target, sems.at[i])
-        for i, (source, target) in enumerate([(pick_hbm, pick), (sup_hbm, sup), (pool_hbm, pool)])
-    ]
-    spots = [block_of((v % blocks) ^ r, LANE) for r in range(blocks)]
-    parts = [
-        pltpu.make_async_copy(dic_hbm.at[at, :], dic.at[at, :], block_sems.at[r])
-        for r, at in enumerate(spots)
-    ]
-    for copy in copies + parts:
-        copy.start()
-    for copy in copies:
-        copy.wait()
-    source = lax.broadcasted_iota(jnp.int32, (pool.shape[0], frames), 0)
-    chosen = jnp.where(source == pick[...], 1.0, 0.0).astype(BF)
-    batch[...] = mm(chosen, pool[...], 0, 0).astype(BF)
     ones = jnp.ones((8, LANE), BF)
     row = lax.broadcasted_iota(jnp.int32, (EXTRA, LANE), 0)
-    for i in range(blocks // 2):
+    for i in range(0, blocks // 2, 2):
         pair = []
-        for r in (2 * i, 2 * i + 1):
-            parts[r].wait()
-            block = dic[spots[r], :] * expand_keep(sup[:, spots[r]], width)
-            masked[spots[r], :] = block
+        for r in (2 * i + odd, 2 * i + 2 + odd):
+            at = block_of((v % blocks) ^ r, LANE)
+            block = dic[at, :] * expand_keep(sup[:, at], width)
+            masked[at, :] = block
             pair.append(block)
         part = mm(batch[...], jnp.concatenate(pair, axis=0), 1, 1)
-        keep[i, :frames, :] = part[:, :LANE]
-        send[i, :frames, :] = part[:, LANE:].astype(BF)
-        for block, out in zip(pair, (keep, send)):
+        for j, block in enumerate(pair):
+            out[i + j, :frames, :] = part[:, j * LANE : (j + 1) * LANE].astype(out.dtype)
             square = jnp.square(block.astype(F32))
             folded = square[:, :LANE]
-            for j in range(1, width // LANE):
-                folded = folded + square[:, j * LANE : (j + 1) * LANE]
+            for k in range(1, width // LANE):
+                folded = folded + square[:, k * LANE : (k + 1) * LANE]
             hi = folded.astype(BF)
             rest = folded - hi.astype(F32)
             mid = rest.astype(BF)
             low = (rest - mid.astype(F32)).astype(BF)
             energy = (mm(ones, hi, 1, 1) + (mm(ones, mid, 1, 1) + mm(ones, low, 1, 1)))[:1]
-            if out is keep:
-                out[i, frames:, :] = jnp.where(row == 0, energy, 0.0)
+            if odd:
+                out[i + j, frames:, :] = split_rows(energy).astype(BF)
             else:
-                out[i, frames:, :] = split_rows(energy).astype(BF)
+                out[i + j, frames:, :] = jnp.where(row == 0, energy, 0.0)
+
+
+def send_part(dic, sup, batch, masked, send):
+    blocks_of(1, dic, sup, batch, masked, send)
+
+
+def keep_part(dic, sup, batch, half, masked, keep):
+    blocks_of(0, dic, sup, batch, masked, keep)
 
 
 def gram_part(masked, keep, send):
@@ -157,9 +162,16 @@
 
 
 def pack(*refs):
-    *parts, out = refs
+    *parts, half, rest = refs
     for i, part in enumerate(parts):
-        out[i] = part[...]
+        half[i] = part[...]
+        if i:
+            rest[i - 1] = part[...]
+
+
+def join(own, rest, half):
+    half[0] = own[...]
+    half[1:] = rest[...]
 
 
 def place(half, other, whole):
@@ -192,7 +204,7 @@
     out[...] = kept * out[...] * scale
 
 
-def call(kernel, outs, args, scratch=(), flops=0, space=pltpu.VMEM):
+def call(kernel, outs, args, scratch=(), flops=0, space=pltpu.VMEM, alias=None):
     moved = sum(a.size * a.dtype.itemsize for a in (*args, *outs))
     single = len(outs) == 1
     return pl.pallas_call(
@@ -203,6 +215,7 @@
         if single
         else [pl.BlockSpec(memory_space=pltpu.VMEM)] * len(outs),
         scratch_shapes=list(scratch),
+        input_output_aliases=alias or {},
         compiler_params=pltpu.CompilerParams(vmem_limit_bytes=8 * 2**20),
         cost_estimate=pl.CostEstimate(flops=flops, bytes_accessed=moved, transcendentals=0),
     )(*args)
@@ -244,25 +257,35 @@
         return mine, gots
 
     sup = support.T
-    batch, masked, keep, send = call(
-        prepare,
-        [
-            shape((frames, width), BF),
-            shape((modes, width), BF),
-            shape((blocks // 2, frames + EXTRA, LANE), F32),
-            shape((blocks // 2, frames + EXTRA, LANE), BF),
-        ],
-        (pool, dictionary, sup, pick.reshape(1, frames)),
+    raw = (pool, dictionary, sup, pick.reshape(1, frames))
+    batch, dic, sup = call(
+        load,
+        [shape((frames, width), BF), shape((modes, width), BF), shape(sup.shape, jnp.int32)],
+        tuple(pltpu.with_memory_space_constraint(x, pltpu.HBM) for x in raw),
         [
             pltpu.VMEM(pool.shape, BF),
-            pltpu.VMEM(dictionary.shape, BF),
-            pltpu.VMEM(sup.shape, jnp.int32),
             pltpu.VMEM((1, frames), jnp.int32),
-            pltpu.SemaphoreType.DMA((3,)),
-            pltpu.SemaphoreType.DMA((blocks,)),
+            pltpu.SemaphoreType.DMA((4,)),
         ],
-        2 * frames * modes * width,
+        2 * frames * pool.shape[0] * width,
         pltpu.HBM,
+    )
+    groups = range(1, n_frame)
+    batches = [hop(batch, "frame", s) for s in groups]
+    half_size = frames * modes * width
+    part = shape((blocks // 2, frames + EXTRA, LANE), F32)
+    masked, send = call(
+        send_part,
+        [shape((modes, width), BF), shape(part.shape, BF)],
+        (dic, sup, batch),
+        flops=half_size,
+    )
+    masked, keep = call(
+        keep_part,
+        [shape((modes, width), BF), part],
+        (dic, sup, batch, masked),
+        flops=half_size,
+        alias={3: 0},
     )
     gram_keep, gram_send = call(
         gram_part,
@@ -296,12 +319,13 @@
         [pltpu.VMEM((modes, LANE), BF)],
         2 * frames * modes * LANE,
     )
-    half = call(
-        pack, [shape((blocks // 2, frames, LANE), BF)], (code, *[hop(code, "vox", m) for m in line])
-    )
-    groups = range(1, n_frame)
-    batches = [hop(batch, "frame", s) for s in groups]
-    halves = [hop(half, "frame", s) for s in groups]
+    own_hops = [hop(code, "frame", s) for s in groups]
+    half, rest = call(
+        pack,
+        [shape((blocks // 2, frames, LANE), BF), shape((blocks // 2 - 1, frames, LANE), BF)],
+        (code, *[hop(code, "vox", m) for m in line]),
+    )
+    halves = [call(join, [half], (o, hop(rest, "frame", s))) for s, o in zip(groups, own_hops)]
     other = hop(half, "vox", 1)
     others = [hop(h, "vox", 1) for h in halves]
     codes, total = call(

time: 96.7 us -> 90.4 us (0.935)
  waiting for transfers between devices: 47.3 us -> 38.9 us
  starting transfers between devices: 32.9 us -> 39.3 us
  local copies, waits for them, and re-layouts: 4.25 us -> 0 us
    ppermute x31 -> x34, waiting for transfers between devices: 47.3 us -> 38.9 us  [hop(): return lax.ppermute(x, axis, [(k, k ^ m) for k in range(n)])]
    ppermute x31 -> x34, starting transfers between devices: 32.9 us -> 39.3 us  [hop(): return lax.ppermute(x, axis, [(k, k ^ m) for k in range(n)])]
    unnamed x10 -> x0, local copies, waits for them, and re-layouts: 4.25 us -> none
    pallas_call x12 -> x17, Pallas kernels: 11.2 us -> 11.1 us  [call(): pl.pallas_call(kernel, out_shape=outs[0] if single else outs, in_specs=[p...]
  transfers between devices with their start and end apart: 31 -> 34, of which waited for: 12 -> 8; matrix products, arithmetic and copies ran while one was open for 0% -> 0% of each run, Pallas kernels for 5% -> 6%
where the time goes in v2:
time: 90.4 us; the launch traced here: 90.1 us
  starting transfers between devices  39.3 us (43%)
  waiting for transfers between devices  38.9 us (43%)
  Pallas kernels  11.1 us (12%)
    ppermute x34, starting transfers between devices, hop(): return lax.ppermute(x, axis, [(k, k ^ m) for k in range(n)])  39.3 us
    ppermute x34, waiting for transfers between devices, hop(): return lax.ppermute(x, axis, [(k, k ^ m) for k in range(n)])  38.9 us
    pallas_call x17, Pallas kernels, call(): pl.pallas_call(kernel, out_shape=outs[0] if single else outs, in_specs=[p...  11.1 us
  transfers between devices with their start and end apart: 34, of which 8 were waited for; matrix products, arithmetic and copies ran while one was open for 0% of the time, Pallas kernels for 6%

profile of v2, /device:TPU:0, one launch (start us, length us, event | category | flops | bytes accessed | tf_op | source)
XLA Modules:
  0.0 90.1 jit_solution(3702377314806965998)
XLA Ops:
  0.6 2.0 %shard_map.59 = (bf16[256,1024]{1,0:T(8,128)(2,1)S(1)}, bf16[1024,1024]{1,0:T(8,128)(2,1)S(1)}, s32[8,1024]{1,0:T(8,128)S(1)}) custom-call(bf16[512,1024]{1,0:T(8,128)(2,1)} %pool_hbm.1, bf16[1024,1024]{1,0:T(8,128)(2,1)} %dic_hbm.1, s32[8,1024]{1,0:T(8,128)} %bitcast.2, s32[1,256]{1,0:T(1,128)} %bitcast.3), custom_call_target="tpu_custom_call" | custom-call | flops 268435456 | bytes 5833728 | tf_op jit(solution)/shard_map/pallas_call | solution.py:210
  2.6 1.2 %shard_map.60 = (bf16[1024,1024]{1,0:T(8,128)(2,1)S(1)}, bf16[4,272,128]{2,1,0:T(8,128)(2,1)S(1)}) custom-call(bf16[1024,1024]{1,0:T(8,128)(2,1)S(1)} %get-tuple-element.26.dic, s32[8,1024]{1,0:T(8,128)S(1)} %get-tuple-element.27.sup, bf16[256,1024]{1,0:T(8,128)(2,1)S(1)} %get-tuple-element.28.batch), custom_call_target="tpu_custom_call" | custom-call | flops 268435456 | bytes 5029888 | tf_op jit(solution)/shard_map/pallas_call | solution.py:210
  6.5 3.0 %collective-permute-start.33 = (bf16[256,1024]{1,0:T(8,128)(2,1)S(1)}, bf16[256,1024]{1,0:T(8,128)(2,1)S(1)}, u32[]{:S(2)}, u32[]{:S(2)}) collective-permute-start(bf16[256,1024]{1,0:T(8,128)(2,1)S(1)} %get-tuple-element.28.batch), channel_id=1, source_target_pairs={{0,8},{8,0},{16,24},{24,16},{1,9},{9,1},{17,25},{25,17},{2,10},{10... | collective-permute-start | bytes 1572872 | tf_op jit(solution)/shard_map/ppermute | solution.py:238
  9.5 1.6 %collective-permute-start.12 = (bf16[256,128]{1,0:T(8,128)(2,1)S(1)}, bf16[256,128]{1,0:T(8,128)(2,1)S(1)}, u32[]{:S(2)}, u32[]{:S(2)}) collective-permute-start(bf16[256,128]{1,0:T(8,128)(2,1)S(1)} %get-tuple-element.41), channel_id=1, source_target_pairs={{0,2},{1,3},{2,0},{3,1},{4,6},{5,7},{6,4},{7,5},{8,10},{9,11},{10,... | collective-permute-start | bytes 196616 | tf_op jit(solution)/shard_map/ppermute | solution.py:238
  11.1 2.6 %collective-permute-start.13 = (bf16[256,128]{1,0:T(8,128)(2,1)S(1)}, bf16[256,128]{1,0:T(8,128)(2,1)S(1)}, u32[]{:S(2)}, u32[]{:S(2)}) collective-permute-start(bf16[256,128]{1,0:T(8,128)(2,1)S(1)} %get-tuple-element.42), channel_id=1, source_target_pairs={{0,4},{1,5},{2,6},{3,7},{4,0},{5,1},{6,2},{7,3},{8,12},{9,13},{10,... | collective-permute-start | bytes 196616 | tf_op jit(solution)/shard_map/ppermute | solution.py:238
  14.3 1.3 %collective-permute-start.14 = (bf16[256,128]{1,0:T(8,128)(2,1)S(1)}, bf16[256,128]{1,0:T(8,128)(2,1)S(1)}, u32[]{:S(2)}, u32[]{:S(2)}) collective-permute-start(bf16[256,128]{1,0:T(8,128)(2,1)S(1)} %get-tuple-element.43), channel_id=1, source_target_pairs={{0,6},{1,7},{2,4},{3,5},{4,2},{5,3},{6,0},{7,1},{8,14},{9,15},{10,... | collective-permute-start | bytes 196616 | tf_op jit(solution)/shard_map/ppermute | solution.py:238
  15.7 1.7 %collective-permute-start.2 = (bf16[272,128]{1,0:T(8,128)(2,1)S(1)}, bf16[272,128]{1,0:T(8,128)(2,1)S(1)}, u32[]{:S(2)}, u32[]{:S(2)}) collective-permute-start(bf16[272,128]{1,0:T(8,128)(2,1)S(1)} %get-tuple-element.34), channel_id=1, source_target_pairs={{0,4},{1,5},{2,6},{3,7},{4,0},{5,1},{6,2},{7,3},{8,12},{9,13},{10,... | collective-permute-start | bytes 208904 | tf_op jit(solution)/shard_map/ppermute | solution.py:238
  17.4 4.4 %collective-permute-start.3 = (bf16[272,128]{1,0:T(8,128)(2,1)S(1)}, bf16[272,128]{1,0:T(8,128)(2,1)S(1)}, u32[]{:S(2)}, u32[]{:S(2)}) collective-permute-start(bf16[272,128]{1,0:T(8,128)(2,1)S(1)} %get-tuple-element.35), channel_id=1, source_target_pairs={{0,6},{1,7},{2,4},{3,5},{4,2},{5,3},{6,0},{7,1},{8,14},{9,15},{10,... | collective-permute-start | bytes 208904 | tf_op jit(solution)/shard_map/ppermute | solution.py:238
  22.4 1.5 %collective-permute-start.16 = (bf16[256,128]{1,0:T(8,128)(2,1)S(1)}, bf16[256,128]{1,0:T(8,128)(2,1)S(1)}, u32[]{:S(2)}, u32[]{:S(2)}) collective-permute-start(bf16[256,128]{1,0:T(8,128)(2,1)S(1)} %shard_map.66.refs_8_), channel_id=1, source_target_pairs={{0,16},{8,24},{16,0},{24,8},{1,17},{9,25},{17,1},{25,9},{2,18},{10... | collective-permute-start | bytes 196616 | tf_op jit(solution)/shard_map/ppermute | solution.py:238
  23.9 1.7 %collective-permute-done.2.rest_1_ = bf16[272,128]{1,0:T(8,128)(2,1)S(1)} collective-permute-done((bf16[272,128]{1,0:T(8,128)(2,1)S(1)}, bf16[272,128]{1,0:T(8,128)(2,1)S(1)}, u32[]{:S(2)}, u32[]{:S(2)}) %collective-permute-start.2) | collective-permute-done | bytes 69664 | tf_op jit(solution)/shard_map/ppermute | solution.py:238
  25.6 2.3 %collective-permute-start.17 = (bf16[256,128]{1,0:T(8,128)(2,1)S(1)}, bf16[256,128]{1,0:T(8,128)(2,1)S(1)}, u32[]{:S(2)}, u32[]{:S(2)}) collective-permute-start(bf16[256,128]{1,0:T(8,128)(2,1)S(1)} %shard_map.66.refs_8_), channel_id=1, source_target_pairs={{0,24},{8,16},{16,8},{24,0},{1,25},{9,17},{17,9},{25,1},{2,26},{10... | collective-permute-start | bytes 196616 | tf_op jit(solution)/shard_map/ppermute | solution.py:238
  27.9 2.2 %collective-permute-start.9 = (bf16[256,128]{1,0:T(8,128)(2,1)S(1)}, bf16[256,128]{1,0:T(8,128)(2,1)S(1)}, u32[]{:S(2)}, u32[]{:S(2)}) collective-permute-start(bf16[256,128]{1,0:T(8,128)(2,1)S(1)} %get-tuple-element.36.refs_0_), channel_id=1, source_target_pairs={{0,6},{1,7},{2,4},{3,5},{4,2},{5,3},{6,0},{7,1},{8,14},{9,15},{10,... | collective-permute-start | bytes 196616 | tf_op jit(solution)/shard_map/ppermute | solution.py:238
  30.2 2.2 %collective-permute-start.7 = (bf16[256,128]{1,0:T(8,128)(2,1)S(1)}, bf16[256,128]{1,0:T(8,128)(2,1)S(1)}, u32[]{:S(2)}, u32[]{:S(2)}) collective-permute-start(bf16[256,128]{1,0:T(8,128)(2,1)S(1)} %get-tuple-element.36.refs_0_), channel_id=1, source_target_pairs={{0,4},{1,5},{2,6},{3,7},{4,0},{5,1},{6,2},{7,3},{8,12},{9,13},{10,... | collective-permute-start | bytes 196616 | tf_op jit(solution)/shard_map/ppermute | solution.py:238
  32.4 1.9 %collective-permute-done.9.refs_6_ = bf16[256,128]{1,0:T(8,128)(2,1)S(1)} collective-permute-done((bf16[256,128]{1,0:T(8,128)(2,1)S(1)}, bf16[256,128]{1,0:T(8,128)(2,1)S(1)}, u32[]{:S(2)}, u32[]{:S(2)}) %collective-permute-start.9) | collective-permute-done | bytes 65568 | tf_op jit(solution)/shard_map/ppermute | solution.py:238
  34.3 1.4 %collective-permute-done.5.refs_2_ = bf16[256,128]{1,0:T(8,128)(2,1)S(1)} collective-permute-done((bf16[256,128]{1,0:T(8,128)(2,1)S(1)}, bf16[256,128]{1,0:T(8,128)(2,1)S(1)}, u32[]{:S(2)}, u32[]{:S(2)}) %collective-permute-start.5) | collective-permute-done | bytes 65568 | tf_op jit(solution)/shard_map/ppermute | solution.py:238
  37.5 1.6 %collective-permute-start.18 = (bf16[256,128]{1,0:T(8,128)(2,1)S(1)}, bf16[256,128]{1,0:T(8,128)(2,1)S(1)}, u32[]{:S(2)}, u32[]{:S(2)}) collective-permute-start(bf16[256,128]{1,0:T(8,128)(2,1)S(1)} %shard_map.67.refs_0_), channel_id=1, source_target_pairs={{0,2},{1,3},{2,0},{3,1},{4,6},{5,7},{6,4},{7,5},{8,10},{9,11},{10,... | collective-permute-start | bytes 196616 | tf_op jit(solution)/shard_map/ppermute | solution.py:238
  40.0 2.0 %collective-permute-start.20 = (bf16[256,128]{1,0:T(8,128)(2,1)S(1)}, bf16[256,128]{1,0:T(8,128)(2,1)S(1)}, u32[]{:S(2)}, u32[]{:S(2)}) collective-permute-start(bf16[256,128]{1,0:T(8,128)(2,1)S(1)} %shard_map.67.refs_0_), channel_id=1, source_target_pairs={{0,6},{1,7},{2,4},{3,5},{4,2},{5,3},{6,0},{7,1},{8,14},{9,15},{10,... | collective-permute-start | bytes 196616 | tf_op jit(solution)/shard_map/ppermute | solution.py:238
  41.9 5.3 %collective-permute-done.19.refs_2_ = bf16[256,128]{1,0:T(8,128)(2,1)S(1)} collective-permute-done((bf16[256,128]{1,0:T(8,128)(2,1)S(1)}, bf16[256,128]{1,0:T(8,128)(2,1)S(1)}, u32[]{:S(2)}, u32[]{:S(2)}) %collective-permute-start.19) | collective-permute-done | bytes 65568 | tf_op jit(solution)/shard_map/ppermute | solution.py:238
  47.6 1.7 %collective-permute-start.30 = (bf16[256,128]{1,0:T(8,128)(2,1)S(1)}, bf16[256,128]{1,0:T(8,128)(2,1)S(1)}, u32[]{:S(2)}, u32[]{:S(2)}) collective-permute-start(bf16[256,128]{1,0:T(8,128)(2,1)S(1)} %shard_map.67.refs_0_), channel_id=1, source_target_pairs={{0,8},{8,0},{16,24},{24,16},{1,9},{9,1},{17,25},{25,17},{2,10},{10... | collective-permute-start | bytes 196616 | tf_op jit(solution)/shard_map/ppermute | solution.py:238
  49.9 1.2 %collective-permute-start.22 = (bf16[256,128]{1,0:T(8,128)(2,1)S(1)}, bf16[256,128]{1,0:T(8,128)(2,1)S(1)}, u32[]{:S(2)}, u32[]{:S(2)}) collective-permute-start(bf16[256,128]{1,0:T(8,128)(2,1)S(1)} %shard_map.67.refs_0_), channel_id=1, source_target_pairs={{0,24},{8,16},{16,8},{24,0},{1,25},{9,17},{17,9},{25,1},{2,26},{10... | collective-permute-start | bytes 196616 | tf_op jit(solution)/shard_map/ppermute | solution.py:238
  52.2 2.3 %collective-permute-done.30.own = bf16[256,128]{1,0:T(8,128)(2,1)S(1)} collective-permute-done((bf16[256,128]{1,0:T(8,128)(2,1)S(1)}, bf16[256,128]{1,0:T(8,128)(2,1)S(1)}, u32[]{:S(2)}, u32[]{:S(2)}) %collective-permute-start.30) | collective-permute-done | bytes 65568 | tf_op jit(solution)/shard_map/ppermute | solution.py:238
  56.5 2.2 %collective-permute-start.23 = (bf16[3,256,128]{2,1,0:T(8,128)(2,1)S(1)}, bf16[3,256,128]{2,1,0:T(8,128)(2,1)S(1)}, u32[]{:S(2)}, u32[]{:S(2)}) collective-permute-start(bf16[3,256,128]{2,1,0:T(8,128)(2,1)S(1)} %get-tuple-element.48), channel_id=1, source_target_pairs={{0,24},{8,16},{16,8},{24,0},{1,25},{9,17},{17,9},{25,1},{2,26},{10... | collective-permute-start | bytes 589832 | tf_op jit(solution)/shard_map/ppermute | solution.py:238
  58.7 25.4 %collective-permute-done.27.rest = bf16[3,256,128]{2,1,0:T(8,128)(2,1)S(1)} collective-permute-done((bf16[3,256,128]{2,1,0:T(8,128)(2,1)S(1)}, bf16[3,256,128]{2,1,0:T(8,128)(2,1)S(1)}, u32[]{:S(2)}, u32[]{:S(2)}) %collective-permute-start.27) | collective-permute-done | bytes 196640 | tf_op jit(solution)/shard_map/ppermute | solution.py:238
  88.0 2.2 %shard_map.75 = f32[256,1024]{1,0:T(8,128)} custom-call(bf16[4,256,128]{2,1,0:T(8,128)(2,1)S(1)} %shard_map.70.half, bf16[4,256,128]{2,1,0:T(8,128)(2,1)S(1)} %collective-permute-done.24.other, bf16[256,1024]{1,0:T(8,128)(2,1)S(1)} %collective-permute-done.25.batch, bf16[1024,1024]{1,0:T(8,128)(2,1)S(1)} %get-tuple-element.37.masked, ...), custom_call_target="tpu_custom_call" | custom-call | flops 671088640 | bytes 5275648 | tf_op jit(solution)/shard_map/pallas_call | solution.py:210
  (61 shorter events, 14.4 us)
Async XLA Ops:
  3.8 9.9 %collective-permute-start = (bf16[4,272,128]{2,1,0:T(8,128)(2,1)S(1)}, bf16[4,272,128]{2,1,0:T(8,128)(2,1)S(1)}, u32[]{:S(2)}, u32[]{:S(2)}) collective-permute-start(bf16[4,272,128]{2,1,0:T(8,128)(2,1)S(1)} %get-tuple-element.31), channel_id=1, source_target_pairs={{0,1},{1,0},{2,3},{3,2},{4,5},{5,4},{6,7},{7,6},{8,9},{9,8},{10,11... | collective-permute-start | bytes 835592 | tf_op jit(solution)/shard_map/ppermute | solution.py:238
  6.5 44.7 %collective-permute-start.33 = (bf16[256,1024]{1,0:T(8,128)(2,1)S(1)}, bf16[256,1024]{1,0:T(8,128)(2,1)S(1)}, u32[]{:S(2)}, u32[]{:S(2)}) collective-permute-start(bf16[256,1024]{1,0:T(8,128)(2,1)S(1)} %get-tuple-element.28.batch), channel_id=1, source_target_pairs={{0,8},{8,0},{16,24},{24,16},{1,9},{9,1},{17,25},{25,17},{2,10},{10... | collective-permute-start | bytes 1572872 | tf_op jit(solution)/shard_map/ppermute | solution.py:238
  9.5 6.2 %collective-permute-start.12 = (bf16[256,128]{1,0:T(8,128)(2,1)S(1)}, bf16[256,128]{1,0:T(8,128)(2,1)S(1)}, u32[]{:S(2)}, u32[]{:S(2)}) collective-permute-start(bf16[256,128]{1,0:T(8,128)(2,1)S(1)} %get-tuple-element.41), channel_id=1, source_target_pairs={{0,2},{1,3},{2,0},{3,1},{4,6},{5,7},{6,4},{7,5},{8,10},{9,11},{10,... | collective-permute-start | bytes 196616 | tf_op jit(solution)/shard_map/ppermute | solution.py:238
  11.1 6.2 %collective-permute-start.13 = (bf16[256,128]{1,0:T(8,128)(2,1)S(1)}, bf16[256,128]{1,0:T(8,128)(2,1)S(1)}, u32[]{:S(2)}, u32[]{:S(2)}) collective-permute-start(bf16[256,128]{1,0:T(8,128)(2,1)S(1)} %get-tuple-element.42), channel_id=1, source_target_pairs={{0,4},{1,5},{2,6},{3,7},{4,0},{5,1},{6,2},{7,3},{8,12},{9,13},{10,... | collective-permute-start | bytes 196616 | tf_op jit(solution)/shard_map/ppermute | solution.py:238
  13.8 8.5 %collective-permute-start.1 = (bf16[272,128]{1,0:T(8,128)(2,1)S(1)}, bf16[272,128]{1,0:T(8,128)(2,1)S(1)}, u32[]{:S(2)}, u32[]{:S(2)}) collective-permute-start(bf16[272,128]{1,0:T(8,128)(2,1)S(1)} %get-tuple-element.33), channel_id=1, source_target_pairs={{0,2},{1,3},{2,0},{3,1},{4,6},{5,7},{6,4},{7,5},{8,10},{9,11},{10,... | collective-permute-start | bytes 208904 | tf_op jit(solution)/shard_map/ppermute | solution.py:238
  14.3 7.4 %collective-permute-start.14 = (bf16[256,128]{1,0:T(8,128)(2,1)S(1)}, bf16[256,128]{1,0:T(8,128)(2,1)S(1)}, u32[]{:S(2)}, u32[]{:S(2)}) collective-permute-start(bf16[256,128]{1,0:T(8,128)(2,1)S(1)} %get-tuple-element.43), channel_id=1, source_target_pairs={{0,6},{1,7},{2,4},{3,5},{4,2},{5,3},{6,0},{7,1},{8,14},{9,15},{10,... | collective-permute-start | bytes 196616 | tf_op jit(solution)/shard_map/ppermute | solution.py:238
  15.7 9.9 %collective-permute-start.2 = (bf16[272,128]{1,0:T(8,128)(2,1)S(1)}, bf16[272,128]{1,0:T(8,128)(2,1)S(1)}, u32[]{:S(2)}, u32[]{:S(2)}) collective-permute-start(bf16[272,128]{1,0:T(8,128)(2,1)S(1)} %get-tuple-element.34), channel_id=1, source_target_pairs={{0,4},{1,5},{2,6},{3,7},{4,0},{5,1},{6,2},{7,3},{8,12},{9,13},{10,... | collective-permute-start | bytes 208904 | tf_op jit(solution)/shard_map/ppermute | solution.py:238
  17.4 10.5 %collective-permute-start.3 = (bf16[272,128]{1,0:T(8,128)(2,1)S(1)}, bf16[272,128]{1,0:T(8,128)(2,1)S(1)}, u32[]{:S(2)}, u32[]{:S(2)}) collective-permute-start(bf16[272,128]{1,0:T(8,128)(2,1)S(1)} %get-tuple-element.35), channel_id=1, source_target_pairs={{0,6},{1,7},{2,4},{3,5},{4,2},{5,3},{6,0},{7,1},{8,14},{9,15},{10,... | collective-permute-start | bytes 208904 | tf_op jit(solution)/shard_map/ppermute | solution.py:238
  21.8 8.4 %collective-permute-start.15 = (bf16[256,128]{1,0:T(8,128)(2,1)S(1)}, bf16[256,128]{1,0:T(8,128)(2,1)S(1)}, u32[]{:S(2)}, u32[]{:S(2)}) collective-permute-start(bf16[256,128]{1,0:T(8,128)(2,1)S(1)} %shard_map.66.refs_8_), channel_id=1, source_target_pairs={{0,8},{8,0},{16,24},{24,16},{1,9},{9,1},{17,25},{25,17},{2,10},{10... | collective-permute-start | bytes 196616 | tf_op jit(solution)/shard_map/ppermute | solution.py:238
  22.4 7.8 %collective-permute-start.16 = (bf16[256,128]{1,0:T(8,128)(2,1)S(1)}, bf16[256,128]{1,0:T(8,128)(2,1)S(1)}, u32[]{:S(2)}, u32[]{:S(2)}) collective-permute-start(bf16[256,128]{1,0:T(8,128)(2,1)S(1)} %shard_map.66.refs_8_), channel_id=1, source_target_pairs={{0,16},{8,24},{16,0},{24,8},{1,17},{9,25},{17,1},{25,9},{2,18},{10... | collective-permute-start | bytes 196616 | tf_op jit(solution)/shard_map/ppermute | solution.py:238
  25.6 6.8 %collective-permute-start.17 = (bf16[256,128]{1,0:T(8,128)(2,1)S(1)}, bf16[256,128]{1,0:T(8,128)(2,1)S(1)}, u32[]{:S(2)}, u32[]{:S(2)}) collective-permute-start(bf16[256,128]{1,0:T(8,128)(2,1)S(1)} %shard_map.66.refs_8_), channel_id=1, source_target_pairs={{0,24},{8,16},{16,8},{24,0},{1,25},{9,17},{17,9},{25,1},{2,26},{10... | collective-permute-start | bytes 196616 | tf_op jit(solution)/shard_map/ppermute | solution.py:238
  27.9 6.4 %collective-permute-start.9 = (bf16[256,128]{1,0:T(8,128)(2,1)S(1)}, bf16[256,128]{1,0:T(8,128)(2,1)S(1)}, u32[]{:S(2)}, u32[]{:S(2)}) collective-permute-start(bf16[256,128]{1,0:T(8,128)(2,1)S(1)} %get-tuple-element.36.refs_0_), channel_id=1, source_target_pairs={{0,6},{1,7},{2,4},{3,5},{4,2},{5,3},{6,0},{7,1},{8,14},{9,15},{10,... | collective-permute-start | bytes 196616 | tf_op jit(solution)/shard_map/ppermute | solution.py:238
  30.2 5.5 %collective-permute-start.5 = (bf16[256,128]{1,0:T(8,128)(2,1)S(1)}, bf16[256,128]{1,0:T(8,128)(2,1)S(1)}, u32[]{:S(2)}, u32[]{:S(2)}) collective-permute-start(bf16[256,128]{1,0:T(8,128)(2,1)S(1)} %get-tuple-element.36.refs_0_), channel_id=1, source_target_pairs={{0,2},{1,3},{2,0},{3,1},{4,6},{5,7},{6,4},{7,5},{8,10},{9,11},{10,... | collective-permute-start | bytes 196616 | tf_op jit(solution)/shard_map/ppermute | solution.py:238
  39.0 8.2 %collective-permute-start.19 = (bf16[256,128]{1,0:T(8,128)(2,1)S(1)}, bf16[256,128]{1,0:T(8,128)(2,1)S(1)}, u32[]{:S(2)}, u32[]{:S(2)}) collective-permute-start(bf16[256,128]{1,0:T(8,128)(2,1)S(1)} %shard_map.67.refs_0_), channel_id=1, source_target_pairs={{0,4},{1,5},{2,6},{3,7},{4,0},{5,1},{6,2},{7,3},{8,12},{9,13},{10,... | collective-permute-start | bytes 196616 | tf_op jit(solution)/shard_map/ppermute | solution.py:238
  40.0 7.3 %collective-permute-start.20 = (bf16[256,128]{1,0:T(8,128)(2,1)S(1)}, bf16[256,128]{1,0:T(8,128)(2,1)S(1)}, u32[]{:S(2)}, u32[]{:S(2)}) collective-permute-start(bf16[256,128]{1,0:T(8,128)(2,1)S(1)} %shard_map.67.refs_0_), channel_id=1, source_target_pairs={{0,6},{1,7},{2,4},{3,5},{4,2},{5,3},{6,0},{7,1},{8,14},{9,15},{10,... | collective-permute-start | bytes 196616 | tf_op jit(solution)/shard_map/ppermute | solution.py:238
  47.3 9.2 %collective-permute-start.31 = (bf16[3,256,128]{2,1,0:T(8,128)(2,1)S(1)}, bf16[3,256,128]{2,1,0:T(8,128)(2,1)S(1)}, u32[]{:S(2)}, u32[]{:S(2)}) collective-permute-start(bf16[3,256,128]{2,1,0:T(8,128)(2,1)S(1)} %get-tuple-element.48), channel_id=1, source_target_pairs={{0,8},{8,0},{16,24},{24,16},{1,9},{9,1},{17,25},{25,17},{2,10},{10... | collective-permute-start | bytes 589832 | tf_op jit(solution)/shard_map/ppermute | solution.py:238
  47.6 6.8 %collective-permute-start.30 = (bf16[256,128]{1,0:T(8,128)(2,1)S(1)}, bf16[256,128]{1,0:T(8,128)(2,1)S(1)}, u32[]{:S(2)}, u32[]{:S(2)}) collective-permute-start(bf16[256,128]{1,0:T(8,128)(2,1)S(1)} %shard_map.67.refs_0_), channel_id=1, source_target_pairs={{0,8},{8,0},{16,24},{24,16},{1,9},{9,1},{17,25},{25,17},{2,10},{10... | collective-permute-start | bytes 196616 | tf_op jit(solution)/shard_map/ppermute | solution.py:238
  49.4 6.3 %collective-permute-start.26 = (bf16[256,128]{1,0:T(8,128)(2,1)S(1)}, bf16[256,128]{1,0:T(8,128)(2,1)S(1)}, u32[]{:S(2)}, u32[]{:S(2)}) collective-permute-start(bf16[256,128]{1,0:T(8,128)(2,1)S(1)} %shard_map.67.refs_0_), channel_id=1, source_target_pairs={{0,16},{8,24},{16,0},{24,8},{1,17},{9,25},{17,1},{25,9},{2,18},{10... | collective-permute-start | bytes 196616 | tf_op jit(solution)/shard_map/ppermute | solution.py:238
  49.9 6.6 %collective-permute-start.22 = (bf16[256,128]{1,0:T(8,128)(2,1)S(1)}, bf16[256,128]{1,0:T(8,128)(2,1)S(1)}, u32[]{:S(2)}, u32[]{:S(2)}) collective-permute-start(bf16[256,128]{1,0:T(8,128)(2,1)S(1)} %shard_map.67.refs_0_), channel_id=1, source_target_pairs={{0,24},{8,16},{16,8},{24,0},{1,25},{9,17},{17,9},{25,1},{2,26},{10... | collective-permute-start | bytes 196616 | tf_op jit(solution)/shard_map/ppermute | solution.py:238
  51.1 35.8 %collective-permute-start.29 = (bf16[256,1024]{1,0:T(8,128)(2,1)S(1)}, bf16[256,1024]{1,0:T(8,128)(2,1)S(1)}, u32[]{:S(2)}, u32[]{:S(2)}) collective-permute-start(bf16[256,1024]{1,0:T(8,128)(2,1)S(1)} %get-tuple-element.28.batch), channel_id=1, source_target_pairs={{0,16},{8,24},{16,0},{24,8},{1,17},{9,25},{17,1},{25,9},{2,18},{10... | collective-permute-start | bytes 1572872 | tf_op jit(solution)/shard_map/ppermute | solution.py:238
  54.5 29.6 %collective-permute-start.27 = (bf16[3,256,128]{2,1,0:T(8,128)(2,1)S(1)}, bf16[3,256,128]{2,1,0:T(8,128)(2,1)S(1)}, u32[]{:S(2)}, u32[]{:S(2)}) collective-permute-start(bf16[3,256,128]{2,1,0:T(8,128)(2,1)S(1)} %get-tuple-element.48), channel_id=1, source_target_pairs={{0,16},{8,24},{16,0},{24,8},{1,17},{9,25},{17,1},{25,9},{2,18},{10... | collective-permute-start | bytes 589832 | tf_op jit(solution)/shard_map/ppermute | solution.py:238
  55.7 32.3 %collective-permute-start.25 = (bf16[256,1024]{1,0:T(8,128)(2,1)S(1)}, bf16[256,1024]{1,0:T(8,128)(2,1)S(1)}, u32[]{:S(2)}, u32[]{:S(2)}) collective-permute-start(bf16[256,1024]{1,0:T(8,128)(2,1)S(1)} %get-tuple-element.28.batch), channel_id=1, source_target_pairs={{0,24},{8,16},{16,8},{24,0},{1,25},{9,17},{17,9},{25,1},{2,26},{10... | collective-permute-start | bytes 1572872 | tf_op jit(solution)/shard_map/ppermute | solution.py:238
  56.5 28.2 %collective-permute-start.21 = (bf16[4,256,128]{2,1,0:T(8,128)(2,1)S(1)}, bf16[4,256,128]{2,1,0:T(8,128)(2,1)S(1)}, u32[]{:S(2)}, u32[]{:S(2)}) collective-permute-start(bf16[4,256,128]{2,1,0:T(8,128)(2,1)S(1)} %get-tuple-element.46.half), channel_id=1, source_target_pairs={{0,1},{1,0},{2,3},{3,2},{4,5},{5,4},{6,7},{7,6},{8,9},{9,8},{10,11... | collective-permute-start | bytes 786440 | tf_op jit(solution)/shard_map/ppermute | solution.py:238
  56.5 27.6 %collective-permute-start.23 = (bf16[3,256,128]{2,1,0:T(8,128)(2,1)S(1)}, bf16[3,256,128]{2,1,0:T(8,128)(2,1)S(1)}, u32[]{:S(2)}, u32[]{:S(2)}) collective-permute-start(bf16[3,256,128]{2,1,0:T(8,128)(2,1)S(1)} %get-tuple-element.48), channel_id=1, source_target_pairs={{0,24},{8,16},{16,8},{24,0},{1,25},{9,17},{17,9},{25,1},{2,26},{10... | collective-permute-start | bytes 589832 | tf_op jit(solution)/shard_map/ppermute | solution.py:238
  (10 other events, 29.3 us)

commit v3 on v2

--- a/solution.py
+++ b/solution.py
@@ -119,10 +119,19 @@
     return jnp.concatenate([total[:top].astype(BF), split_rows(energy).astype(BF)], axis=0)
 
 
-def fold_core(extra, keep, got, own, *sends):
+def fold_core(keep, got, own, *sends):
     own[...] = keep[0] + got[0].astype(F32)
     for i, out in enumerate(sends):
-        out[...] = pack_sum(keep[i + 1] + got[i + 1].astype(F32), extra)
+        out[...] = pack_sum(keep[i + 1] + got[i + 1].astype(F32), EXTRA)
+
+
+def fold_half(keep, got, left, sent):
+    for i in range(keep.shape[0]):
+        total = keep[i] + got[i].astype(F32)
+        if i % 2:
+            sent[i // 2] = total.astype(BF)
+        else:
+            left[i // 2] = total
 
 
 def fold_line(own, *rest):
@@ -182,12 +191,13 @@
         whole[:, block_of((v % (2 * count)) ^ (2 * i + 1), LANE)] = other[i]
 
 
-def own_group(half, other, masked, batch, codes, total):
+def own_group(half, other, masked, batch, sup, codes, total, kept):
     f = lax.axis_index("frame")
     place(half, other, codes)
     error = (mm(codes[...], masked[...], 1, 0) - batch[...].astype(F32)).astype(BF)
     rows = total.shape[0]
     total[...] = mm(codes[:, block_of(f, rows)], error, 0, 0)
+    kept[...] = expand_keep(sup[:, block_of(f, rows)], total.shape[1])
 
 
 def add_group(half, other, batch, masked, total, out, codes):
@@ -197,23 +207,33 @@
     out[...] = total[...] + mm(codes[:, block_of(f, total.shape[0])], error, 0, 0)
 
 
-def last_group(scale, half, other, batch, masked, total, sup, out, codes):
+def last_group(scale, half, other, batch, masked, total, kept, out_hbm, codes, out, sems):
     f = lax.axis_index("frame")
-    add_group(half, other, batch, masked, total, out, codes)
-    kept = expand_keep(sup[:, block_of(f, total.shape[0])], total.shape[1]).astype(F32)
-    out[...] = kept * out[...] * scale
-
-
-def call(kernel, outs, args, scratch=(), flops=0, space=pltpu.VMEM, alias=None):
+    place(half, other, codes)
+    rows, width = total.shape
+    step = width // sems.shape[0]
+    copies = []
+    for i in range(sems.shape[0]):
+        at = slice(i * step, (i + 1) * step)
+        error = (mm(codes[...], masked[:, at], 1, 0) - batch[:, at].astype(F32)).astype(BF)
+        acc = total[:, at] + mm(codes[:, block_of(f, rows)], error, 0, 0)
+        out[:, at] = kept[:, at].astype(F32) * acc * scale
+        copies.append(pltpu.make_async_copy(out.at[:, at], out_hbm.at[:, at], sems.at[i]))
+        copies[-1].start()
+    for copy in copies:
+        copy.wait()
+
+
+def call(kernel, outs, args, scratch=(), flops=0, space=pltpu.VMEM, alias=None, to=pltpu.VMEM):
     moved = sum(a.size * a.dtype.itemsize for a in (*args, *outs))
     single = len(outs) == 1
     return pl.pallas_call(
         kernel,
         out_shape=outs[0] if single else outs,
         in_specs=[pl.BlockSpec(memory_space=space)] * len(args),
-        out_specs=pl.BlockSpec(memory_space=pltpu.VMEM)
+        out_specs=pl.BlockSpec(memory_space=to)
         if single
-        else [pl.BlockSpec(memory_space=pltpu.VMEM)] * len(outs),
+        else [pl.BlockSpec(memory_space=to)] * len(outs),
         scratch_shapes=list(scratch),
         input_output_aliases=alias or {},
         compiler_params=pltpu.CompilerParams(vmem_limit_bytes=8 * 2**20),
@@ -237,15 +257,7 @@
         n = n_vox if axis == "vox" else n_frame
         return lax.ppermute(x, axis, [(k, k ^ m) for k in range(n)])
 
-    def reduce(keep, send, extra):
-        tall = keep.shape[1]
-        got = hop(send, "vox", 1)
-        mine, *sends = call(
-            functools.partial(fold_core, extra),
-            [shape((tall, LANE), F32)] + [shape((tall, LANE), BF)] * len(line),
-            (keep, got),
-        )
-        gots = [hop(s, "vox", m) for s, m in zip(sends, line)]
+    def across(mine, gots, extra):
         far = blocks
         while far < n_vox:
             total = mine
@@ -296,7 +308,14 @@
         (masked,),
         flops=2 * own * modes * width,
     )
-    mine, gots = reduce(keep, send, EXTRA)
+    tall = frames + EXTRA
+    mine, *sends = call(
+        fold_core,
+        [shape((tall, LANE), F32)] + [shape((tall, LANE), BF)] * len(line),
+        (keep, hop(send, "vox", 1)),
+    )
+    gots = [hop(s, "vox", m) for s, m in zip(sends, line)]
+    mine, gots = across(mine, gots, EXTRA)
     first, corr, step = call(
         fold_line,
         [
@@ -306,7 +325,15 @@
         ],
         (mine, *gots),
     )
-    mine, gots = reduce(gram_keep, gram_send, 0)
+    mask = 1
+    while gram_keep.shape[0] > 1:
+        some = (gram_keep.shape[0] // 2, own, LANE)
+        gram_keep, gram_send = call(
+            fold_half, [shape(some, F32), shape(some, BF)], (gram_keep, hop(gram_send, "vox", mask))
+        )
+        mask *= 2
+    gots = [hop(gram_send[0], "vox", mask)]
+    mine, gots = across(gram_keep[0], gots, 0)
     gram = call(fold_gram, [shape((own, LANE), BF)], (mine, *gots))
     firsts = [first] + [hop(first, "vox", m) for m in line]
     grams = [gram] + [hop(gram, "frame", s) for s in range(1, n_frame)]
@@ -328,10 +355,10 @@
     halves = [call(join, [half], (o, hop(rest, "frame", s))) for s, o in zip(groups, own_hops)]
     other = hop(half, "vox", 1)
     others = [hop(h, "vox", 1) for h in halves]
-    codes, total = call(
+    codes, total, kept = call(
         own_group,
-        [shape((frames, modes), BF), shape((own, width), F32)],
-        (half, other, masked, batch),
+        [shape((frames, modes), BF), shape((own, width), F32), shape((own, width), BF)],
+        (half, other, masked, batch, sup),
         flops=2 * frames * modes * width,
     )
     held = [pltpu.VMEM((frames, modes), BF)]
@@ -344,9 +371,10 @@
             total = call(
                 functools.partial(last_group, 1.0 / (frames * n_frame)),
                 [shape((own, width), F32)],
-                (*args, sup),
-                held,
+                (*args, kept),
+                [*held, pltpu.VMEM((own, width), F32), pltpu.SemaphoreType.DMA((4,))],
                 work_size,
+                to=pltpu.HBM,
             )
     return codes, total
 

time: 90.4 us -> 90.3 us (level)
  starting transfers between devices: 39.3 us -> 31.7 us
  waiting for transfers between devices: 38.9 us -> 45.7 us
    ppermute x34 -> x33, starting transfers between devices: 39.3 us -> 31.7 us  [hop(): return lax.ppermute(x, axis, [(k, k ^ m) for k in range(n)])]
    ppermute x34 -> x33, waiting for transfers between devices: 38.9 us -> 45.7 us  [hop(): return lax.ppermute(x, axis, [(k, k ^ m) for k in range(n)])]
    pallas_call x17 -> x18, Pallas kernels: 11.1 us -> 11.9 us  [call(): pl.pallas_call(kernel, out_shape=outs[0] if single else outs, in_specs=[p...]
  transfers between devices with their start and end apart: 34 -> 33, of which waited for: 8 -> 14; matrix products, arithmetic and copies ran while one was open for 0% -> 0% of each run, Pallas kernels for 6% -> 7%
where the time goes in v3:
time: 90.3 us; the launch traced here: 90.1 us
  waiting for transfers between devices  45.7 us (51%)
  starting transfers between devices  31.7 us (35%)
  Pallas kernels  11.9 us (13%)
    ppermute x33, waiting for transfers between devices, hop(): return lax.ppermute(x, axis, [(k, k ^ m) for k in range(n)])  45.7 us
    ppermute x33, starting transfers between devices, hop(): return lax.ppermute(x, axis, [(k, k ^ m) for k in range(n)])  31.7 us
    pallas_call x18, Pallas kernels, call(): pl.pallas_call(kernel, out_shape=outs[0] if single else outs, in_specs=[p...  11.9 us
  transfers between devices with their start and end apart: 33, of which 14 were waited for; matrix products, arithmetic and copies ran while one was open for 0% of the time, Pallas kernels for 7%

profile of v3, /device:TPU:0, one launch (start us, length us, event | category | flops | bytes accessed | tf_op | source)
XLA Modules:
  0.0 90.1 jit_solution(8917687387559588220)
XLA Ops:
  0.6 2.0 %shard_map.59 = (bf16[256,1024]{1,0:T(8,128)(2,1)S(1)}, bf16[1024,1024]{1,0:T(8,128)(2,1)S(1)}, s32[8,1024]{1,0:T(8,128)S(1)}) custom-call(bf16[512,1024]{1,0:T(8,128)(2,1)} %pool_hbm.1, bf16[1024,1024]{1,0:T(8,128)(2,1)} %dic_hbm.1, s32[8,1024]{1,0:T(8,128)} %bitcast.6, s32[1,256]{1,0:T(1,128)} %bitcast.7), custom_call_target="tpu_custom_call" | custom-call | flops 268435456 | bytes 5833728 | tf_op jit(solution)/shard_map/pallas_call | solution.py:230
  2.6 1.2 %shard_map.60 = (bf16[1024,1024]{1,0:T(8,128)(2,1)S(1)}, bf16[4,272,128]{2,1,0:T(8,128)(2,1)S(1)}) custom-call(bf16[1024,1024]{1,0:T(8,128)(2,1)S(1)} %get-tuple-element.27.dic, s32[8,1024]{1,0:T(8,128)S(1)} %get-tuple-element.28.sup, bf16[256,1024]{1,0:T(8,128)(2,1)S(1)} %get-tuple-element.29.batch), custom_call_target="tpu_custom_call" | custom-call | flops 268435456 | bytes 5029888 | tf_op jit(solution)/shard_map/pallas_call | solution.py:230
  4.4 1.2 %shard_map.61 = (bf16[1024,1024]{1,0:T(8,128)(2,1)S(1)}, f32[4,272,128]{2,1,0:T(8,128)S(1)}) custom-call(bf16[1024,1024]{1,0:T(8,128)(2,1)S(1)} %get-tuple-element.27.dic, s32[8,1024]{1,0:T(8,128)S(1)} %get-tuple-element.28.sup, bf16[256,1024]{1,0:T(8,128)(2,1)S(1)} %get-tuple-element.29.batch, ...), custom_call_target="tpu_custom_call", output_to_operand_aliasing={{0}: (3, {})} | custom-call | flops 268435456 | bytes 7405568 | tf_op jit(solution)/shard_map/pallas_call | solution.py:230
  6.5 3.0 %collective-permute-start.32 = (bf16[256,1024]{1,0:T(8,128)(2,1)S(1)}, bf16[256,1024]{1,0:T(8,128)(2,1)S(1)}, u32[]{:S(2)}, u32[]{:S(2)}) collective-permute-start(bf16[256,1024]{1,0:T(8,128)(2,1)S(1)} %get-tuple-element.29.batch), channel_id=1, source_target_pairs={{0,8},{8,0},{16,24},{24,16},{1,9},{9,1},{17,25},{25,17},{2,10},{10... | collective-permute-start | bytes 1572872 | tf_op jit(solution)/shard_map/ppermute | solution.py:258
  9.5 1.6 %collective-permute-start.1 = (bf16[272,128]{1,0:T(8,128)(2,1)S(1)}, bf16[272,128]{1,0:T(8,128)(2,1)S(1)}, u32[]{:S(2)}, u32[]{:S(2)}) collective-permute-start(bf16[272,128]{1,0:T(8,128)(2,1)S(1)} %get-tuple-element.34), channel_id=1, source_target_pairs={{0,2},{1,3},{2,0},{3,1},{4,6},{5,7},{6,4},{7,5},{8,10},{9,11},{10,... | collective-permute-start | bytes 208904 | tf_op jit(solution)/shard_map/ppermute | solution.py:258
  11.2 2.6 %collective-permute-start.2 = (bf16[272,128]{1,0:T(8,128)(2,1)S(1)}, bf16[272,128]{1,0:T(8,128)(2,1)S(1)}, u32[]{:S(2)}, u32[]{:S(2)}) collective-permute-start(bf16[272,128]{1,0:T(8,128)(2,1)S(1)} %get-tuple-element.35), channel_id=1, source_target_pairs={{0,4},{1,5},{2,6},{3,7},{4,0},{5,1},{6,2},{7,3},{8,12},{9,13},{10,... | collective-permute-start | bytes 208904 | tf_op jit(solution)/shard_map/ppermute | solution.py:258
  14.8 3.9 %collective-permute-done.2.rest_1_ = bf16[272,128]{1,0:T(8,128)(2,1)S(1)} collective-permute-done((bf16[272,128]{1,0:T(8,128)(2,1)S(1)}, bf16[272,128]{1,0:T(8,128)(2,1)S(1)}, u32[]{:S(2)}, u32[]{:S(2)}) %collective-permute-start.2) | collective-permute-done | bytes 69664 | tf_op jit(solution)/shard_map/ppermute | solution.py:258
  18.7 1.6 %collective-permute-done.3.rest_2_ = bf16[272,128]{1,0:T(8,128)(2,1)S(1)} collective-permute-done((bf16[272,128]{1,0:T(8,128)(2,1)S(1)}, bf16[272,128]{1,0:T(8,128)(2,1)S(1)}, u32[]{:S(2)}, u32[]{:S(2)}) %collective-permute-start.3) | collective-permute-done | bytes 69664 | tf_op jit(solution)/shard_map/ppermute | solution.py:258
  20.3 1.9 %collective-permute-start.9 = (bf16[256,128]{1,0:T(8,128)(2,1)S(1)}, bf16[256,128]{1,0:T(8,128)(2,1)S(1)}, u32[]{:S(2)}, u32[]{:S(2)}) collective-permute-start(bf16[256,128]{1,0:T(8,128)(2,1)S(1)} %get-tuple-element.37.refs_0_), channel_id=1, source_target_pairs={{0,6},{1,7},{2,4},{3,5},{4,2},{5,3},{6,0},{7,1},{8,14},{9,15},{10,... | collective-permute-start | bytes 196616 | tf_op jit(solution)/shard_map/ppermute | solution.py:258
  22.4 2.4 %collective-permute-start.7 = (bf16[256,128]{1,0:T(8,128)(2,1)S(1)}, bf16[256,128]{1,0:T(8,128)(2,1)S(1)}, u32[]{:S(2)}, u32[]{:S(2)}) collective-permute-start(bf16[256,128]{1,0:T(8,128)(2,1)S(1)} %get-tuple-element.37.refs_0_), channel_id=1, source_target_pairs={{0,4},{1,5},{2,6},{3,7},{4,0},{5,1},{6,2},{7,3},{8,12},{9,13},{10,... | collective-permute-start | bytes 196616 | tf_op jit(solution)/shard_map/ppermute | solution.py:258
  26.6 2.3 %collective-permute-done.5.refs_2_ = bf16[256,128]{1,0:T(8,128)(2,1)S(1)} collective-permute-done((bf16[256,128]{1,0:T(8,128)(2,1)S(1)}, bf16[256,128]{1,0:T(8,128)(2,1)S(1)}, u32[]{:S(2)}, u32[]{:S(2)}) %collective-permute-start.5) | collective-permute-done | bytes 65568 | tf_op jit(solution)/shard_map/ppermute | solution.py:258
  31.1 1.5 %collective-permute-start.15 = (bf16[256,128]{1,0:T(8,128)(2,1)S(1)}, bf16[256,128]{1,0:T(8,128)(2,1)S(1)}, u32[]{:S(2)}, u32[]{:S(2)}) collective-permute-start(bf16[256,128]{1,0:T(8,128)(2,1)S(1)} %shard_map.67.refs_8_), channel_id=1, source_target_pairs={{0,16},{8,24},{16,0},{24,8},{1,17},{9,25},{17,1},{25,9},{2,18},{10... | collective-permute-start | bytes 196616 | tf_op jit(solution)/shard_map/ppermute | solution.py:258
  32.6 1.4 %collective-permute-start.16 = (bf16[256,128]{1,0:T(8,128)(2,1)S(1)}, bf16[256,128]{1,0:T(8,128)(2,1)S(1)}, u32[]{:S(2)}, u32[]{:S(2)}) collective-permute-start(bf16[256,128]{1,0:T(8,128)(2,1)S(1)} %shard_map.67.refs_8_), channel_id=1, source_target_pairs={{0,24},{8,16},{16,8},{24,0},{1,25},{9,17},{17,9},{25,1},{2,26},{10... | collective-permute-start | bytes 196616 | tf_op jit(solution)/shard_map/ppermute | solution.py:258
  35.4 2.4 %collective-permute-done.16.refs_11_ = bf16[256,128]{1,0:T(8,128)(2,1)S(1)} collective-permute-done((bf16[256,128]{1,0:T(8,128)(2,1)S(1)}, bf16[256,128]{1,0:T(8,128)(2,1)S(1)}, u32[]{:S(2)}, u32[]{:S(2)}) %collective-permute-start.16) | collective-permute-done | bytes 65568 | tf_op jit(solution)/shard_map/ppermute | solution.py:258
  38.2 2.8 %collective-permute-start.18 = (bf16[256,128]{1,0:T(8,128)(2,1)S(1)}, bf16[256,128]{1,0:T(8,128)(2,1)S(1)}, u32[]{:S(2)}, u32[]{:S(2)}) collective-permute-start(bf16[256,128]{1,0:T(8,128)(2,1)S(1)} %shard_map.68.refs_0_), channel_id=1, source_target_pairs={{0,4},{1,5},{2,6},{3,7},{4,0},{5,1},{6,2},{7,3},{8,12},{9,13},{10,... | collective-permute-start | bytes 196616 | tf_op jit(solution)/shard_map/ppermute | solution.py:258
  40.9 1.6 %collective-permute-start.19 = (bf16[256,128]{1,0:T(8,128)(2,1)S(1)}, bf16[256,128]{1,0:T(8,128)(2,1)S(1)}, u32[]{:S(2)}, u32[]{:S(2)}) collective-permute-start(bf16[256,128]{1,0:T(8,128)(2,1)S(1)} %shard_map.68.refs_0_), channel_id=1, source_target_pairs={{0,6},{1,7},{2,4},{3,5},{4,2},{5,3},{6,0},{7,1},{8,14},{9,15},{10,... | collective-permute-start | bytes 196616 | tf_op jit(solution)/shard_map/ppermute | solution.py:258
  43.7 3.3 %collective-permute-done.19.refs_3_ = bf16[256,128]{1,0:T(8,128)(2,1)S(1)} collective-permute-done((bf16[256,128]{1,0:T(8,128)(2,1)S(1)}, bf16[256,128]{1,0:T(8,128)(2,1)S(1)}, u32[]{:S(2)}, u32[]{:S(2)}) %collective-permute-start.19) | collective-permute-done | bytes 65568 | tf_op jit(solution)/shard_map/ppermute | solution.py:258
  47.0 1.6 %collective-permute-start.30 = (bf16[3,256,128]{2,1,0:T(8,128)(2,1)S(1)}, bf16[3,256,128]{2,1,0:T(8,128)(2,1)S(1)}, u32[]{:S(2)}, u32[]{:S(2)}) collective-permute-start(bf16[3,256,128]{2,1,0:T(8,128)(2,1)S(1)} %get-tuple-element.49), channel_id=1, source_target_pairs={{0,8},{8,0},{16,24},{24,16},{1,9},{9,1},{17,25},{25,17},{2,10},{10... | collective-permute-start | bytes 589832 | tf_op jit(solution)/shard_map/ppermute | solution.py:258
  49.6 2.4 %collective-permute-start.21 = (bf16[256,128]{1,0:T(8,128)(2,1)S(1)}, bf16[256,128]{1,0:T(8,128)(2,1)S(1)}, u32[]{:S(2)}, u32[]{:S(2)}) collective-permute-start(bf16[256,128]{1,0:T(8,128)(2,1)S(1)} %shard_map.68.refs_0_), channel_id=1, source_target_pairs={{0,24},{8,16},{16,8},{24,0},{1,25},{9,17},{17,9},{25,1},{2,26},{10... | collective-permute-start | bytes 196616 | tf_op jit(solution)/shard_map/ppermute | solution.py:258
  54.1 6.3 %collective-permute-done.25.own = bf16[256,128]{1,0:T(8,128)(2,1)S(1)} collective-permute-done((bf16[256,128]{1,0:T(8,128)(2,1)S(1)}, bf16[256,128]{1,0:T(8,128)(2,1)S(1)}, u32[]{:S(2)}, u32[]{:S(2)}) %collective-permute-start.25) | collective-permute-done | bytes 65568 | tf_op jit(solution)/shard_map/ppermute | solution.py:258
  60.8 2.7 %collective-permute-start.22 = (bf16[3,256,128]{2,1,0:T(8,128)(2,1)S(1)}, bf16[3,256,128]{2,1,0:T(8,128)(2,1)S(1)}, u32[]{:S(2)}, u32[]{:S(2)}) collective-permute-start(bf16[3,256,128]{2,1,0:T(8,128)(2,1)S(1)} %get-tuple-element.49), channel_id=1, source_target_pairs={{0,24},{8,16},{16,8},{24,0},{1,25},{9,17},{17,9},{25,1},{2,26},{10... | collective-permute-start | bytes 589832 | tf_op jit(solution)/shard_map/ppermute | solution.py:258
  63.4 19.8 %collective-permute-done.26.rest = bf16[3,256,128]{2,1,0:T(8,128)(2,1)S(1)} collective-permute-done((bf16[3,256,128]{2,1,0:T(8,128)(2,1)S(1)}, bf16[3,256,128]{2,1,0:T(8,128)(2,1)S(1)}, u32[]{:S(2)}, u32[]{:S(2)}) %collective-permute-start.26) | collective-permute-done | bytes 196640 | tf_op jit(solution)/shard_map/ppermute | solution.py:258
  84.0 1.2 %shard_map.70 = (bf16[256,1024]{1,0:T(8,128)(2,1)}, f32[256,1024]{1,0:T(8,128)S(1)}, bf16[256,1024]{1,0:T(8,128)(2,1)S(1)}) custom-call(bf16[4,256,128]{2,1,0:T(8,128)(2,1)S(1)} %get-tuple-element.47.half, bf16[4,256,128]{2,1,0:T(8,128)(2,1)S(1)} %collective-permute-done.20.other, bf16[1024,1024]{1,0:T(8,128)(2,1)S(1)} %get-tuple-element.38.masked, ...), custom_call_target="tpu_custom_call" | custom-call | flops 536870912 | bytes 5275648 | tf_op jit(solution)/shard_map/pallas_call | solution.py:230
  87.3 2.9 %shard_map.76 = f32[256,1024]{1,0:T(8,128)} custom-call(bf16[4,256,128]{2,1,0:T(8,128)(2,1)S(1)} %shard_map.71.half, bf16[4,256,128]{2,1,0:T(8,128)(2,1)S(1)} %collective-permute-done.23.other, bf16[256,1024]{1,0:T(8,128)(2,1)S(1)} %collective-permute-done.24.batch, bf16[1024,1024]{1,0:T(8,128)(2,1)S(1)} %get-tuple-element.38.masked, ...), custom_call_target="tpu_custom_call" | custom-call | flops 671088640 | bytes 5767168 | tf_op jit(solution)/shard_map/pallas_call | solution.py:230
  (60 shorter events, 15.8 us)
Async XLA Ops:
  3.8 5.6 %collective-permute-start = (bf16[4,272,128]{2,1,0:T(8,128)(2,1)S(1)}, bf16[4,272,128]{2,1,0:T(8,128)(2,1)S(1)}, u32[]{:S(2)}, u32[]{:S(2)}) collective-permute-start(bf16[4,272,128]{2,1,0:T(8,128)(2,1)S(1)} %get-tuple-element.32), channel_id=1, source_target_pairs={{0,1},{1,0},{2,3},{3,2},{4,5},{5,4},{6,7},{7,6},{8,9},{9,8},{10,11... | collective-permute-start | bytes 835592 | tf_op jit(solution)/shard_map/ppermute | solution.py:258
  6.4 7.6 %collective-permute-start.11 = (bf16[4,256,128]{2,1,0:T(8,128)(2,1)S(1)}, bf16[4,256,128]{2,1,0:T(8,128)(2,1)S(1)}, u32[]{:S(2)}, u32[]{:S(2)}) collective-permute-start(bf16[4,256,128]{2,1,0:T(8,128)(2,1)S(1)} %get-tuple-element.40), channel_id=1, source_target_pairs={{0,1},{1,0},{2,3},{3,2},{4,5},{5,4},{6,7},{7,6},{8,9},{9,8},{10,11... | collective-permute-start | bytes 786440 | tf_op jit(solution)/shard_map/ppermute | solution.py:258
  6.5 45.6 %collective-permute-start.32 = (bf16[256,1024]{1,0:T(8,128)(2,1)S(1)}, bf16[256,1024]{1,0:T(8,128)(2,1)S(1)}, u32[]{:S(2)}, u32[]{:S(2)}) collective-permute-start(bf16[256,1024]{1,0:T(8,128)(2,1)S(1)} %get-tuple-element.29.batch), channel_id=1, source_target_pairs={{0,8},{8,0},{16,24},{24,16},{1,9},{9,1},{17,25},{25,17},{2,10},{10... | collective-permute-start | bytes 1572872 | tf_op jit(solution)/shard_map/ppermute | solution.py:258
  9.5 5.2 %collective-permute-start.1 = (bf16[272,128]{1,0:T(8,128)(2,1)S(1)}, bf16[272,128]{1,0:T(8,128)(2,1)S(1)}, u32[]{:S(2)}, u32[]{:S(2)}) collective-permute-start(bf16[272,128]{1,0:T(8,128)(2,1)S(1)} %get-tuple-element.34), channel_id=1, source_target_pairs={{0,2},{1,3},{2,0},{3,1},{4,6},{5,7},{6,4},{7,5},{8,10},{9,11},{10,... | collective-permute-start | bytes 208904 | tf_op jit(solution)/shard_map/ppermute | solution.py:258
  11.2 7.5 %collective-permute-start.2 = (bf16[272,128]{1,0:T(8,128)(2,1)S(1)}, bf16[272,128]{1,0:T(8,128)(2,1)S(1)}, u32[]{:S(2)}, u32[]{:S(2)}) collective-permute-start(bf16[272,128]{1,0:T(8,128)(2,1)S(1)} %get-tuple-element.35), channel_id=1, source_target_pairs={{0,4},{1,5},{2,6},{3,7},{4,0},{5,1},{6,2},{7,3},{8,12},{9,13},{10,... | collective-permute-start | bytes 208904 | tf_op jit(solution)/shard_map/ppermute | solution.py:258
  13.8 6.5 %collective-permute-start.3 = (bf16[272,128]{1,0:T(8,128)(2,1)S(1)}, bf16[272,128]{1,0:T(8,128)(2,1)S(1)}, u32[]{:S(2)}, u32[]{:S(2)}) collective-permute-start(bf16[272,128]{1,0:T(8,128)(2,1)S(1)} %get-tuple-element.36), channel_id=1, source_target_pairs={{0,6},{1,7},{2,4},{3,5},{4,2},{5,3},{6,0},{7,1},{8,14},{9,15},{10,... | collective-permute-start | bytes 208904 | tf_op jit(solution)/shard_map/ppermute | solution.py:258
  14.0 10.8 %collective-permute-start.12 = (bf16[2,256,128]{2,1,0:T(8,128)(2,1)S(1)}, bf16[2,256,128]{2,1,0:T(8,128)(2,1)S(1)}, u32[]{:S(2)}, u32[]{:S(2)}) collective-permute-start(bf16[2,256,128]{2,1,0:T(8,128)(2,1)S(1)} %get-tuple-element.42), channel_id=1, source_target_pairs={{0,2},{1,3},{2,0},{3,1},{4,6},{5,7},{6,4},{7,5},{8,10},{9,11},{10,... | collective-permute-start | bytes 393224 | tf_op jit(solution)/shard_map/ppermute | solution.py:258
  20.3 6.2 %collective-permute-start.9 = (bf16[256,128]{1,0:T(8,128)(2,1)S(1)}, bf16[256,128]{1,0:T(8,128)(2,1)S(1)}, u32[]{:S(2)}, u32[]{:S(2)}) collective-permute-start(bf16[256,128]{1,0:T(8,128)(2,1)S(1)} %get-tuple-element.37.refs_0_), channel_id=1, source_target_pairs={{0,6},{1,7},{2,4},{3,5},{4,2},{5,3},{6,0},{7,1},{8,14},{9,15},{10,... | collective-permute-start | bytes 196616 | tf_op jit(solution)/shard_map/ppermute | solution.py:258
  22.2 6.7 %collective-permute-start.5 = (bf16[256,128]{1,0:T(8,128)(2,1)S(1)}, bf16[256,128]{1,0:T(8,128)(2,1)S(1)}, u32[]{:S(2)}, u32[]{:S(2)}) collective-permute-start(bf16[256,128]{1,0:T(8,128)(2,1)S(1)} %get-tuple-element.37.refs_0_), channel_id=1, source_target_pairs={{0,2},{1,3},{2,0},{3,1},{4,6},{5,7},{6,4},{7,5},{8,10},{9,11},{10,... | collective-permute-start | bytes 196616 | tf_op jit(solution)/shard_map/ppermute | solution.py:258
  22.4 7.3 %collective-permute-start.7 = (bf16[256,128]{1,0:T(8,128)(2,1)S(1)}, bf16[256,128]{1,0:T(8,128)(2,1)S(1)}, u32[]{:S(2)}, u32[]{:S(2)}) collective-permute-start(bf16[256,128]{1,0:T(8,128)(2,1)S(1)} %get-tuple-element.37.refs_0_), channel_id=1, source_target_pairs={{0,4},{1,5},{2,6},{3,7},{4,0},{5,1},{6,2},{7,3},{8,12},{9,13},{10,... | collective-permute-start | bytes 196616 | tf_op jit(solution)/shard_map/ppermute | solution.py:258
  24.8 5.6 %collective-permute-start.13 = (bf16[256,128]{1,0:T(8,128)(2,1)S(1)}, bf16[256,128]{1,0:T(8,128)(2,1)S(1)}, u32[]{:S(2)}, u32[]{:S(2)}) collective-permute-start(bf16[256,128]{1,0:T(8,128)(2,1)S(1)} %bitcast.5), channel_id=1, source_target_pairs={{0,4},{1,5},{2,6},{3,7},{4,0},{5,1},{6,2},{7,3},{8,12},{9,13},{10,... | collective-permute-start | bytes 196616 | tf_op jit(solution)/shard_map/ppermute | solution.py:258
  30.5 4.6 %collective-permute-start.14 = (bf16[256,128]{1,0:T(8,128)(2,1)S(1)}, bf16[256,128]{1,0:T(8,128)(2,1)S(1)}, u32[]{:S(2)}, u32[]{:S(2)}) collective-permute-start(bf16[256,128]{1,0:T(8,128)(2,1)S(1)} %shard_map.67.refs_8_), channel_id=1, source_target_pairs={{0,8},{8,0},{16,24},{24,16},{1,9},{9,1},{17,25},{25,17},{2,10},{10... | collective-permute-start | bytes 196616 | tf_op jit(solution)/shard_map/ppermute | solution.py:258
  32.6 5.2 %collective-permute-start.16 = (bf16[256,128]{1,0:T(8,128)(2,1)S(1)}, bf16[256,128]{1,0:T(8,128)(2,1)S(1)}, u32[]{:S(2)}, u32[]{:S(2)}) collective-permute-start(bf16[256,128]{1,0:T(8,128)(2,1)S(1)} %shard_map.67.refs_8_), channel_id=1, source_target_pairs={{0,24},{8,16},{16,8},{24,0},{1,25},{9,17},{17,9},{25,1},{2,26},{10... | collective-permute-start | bytes 196616 | tf_op jit(solution)/shard_map/ppermute | solution.py:258
  38.2 5.5 %collective-permute-start.18 = (bf16[256,128]{1,0:T(8,128)(2,1)S(1)}, bf16[256,128]{1,0:T(8,128)(2,1)S(1)}, u32[]{:S(2)}, u32[]{:S(2)}) collective-permute-start(bf16[256,128]{1,0:T(8,128)(2,1)S(1)} %shard_map.68.refs_0_), channel_id=1, source_target_pairs={{0,4},{1,5},{2,6},{3,7},{4,0},{5,1},{6,2},{7,3},{8,12},{9,13},{10,... | collective-permute-start | bytes 196616 | tf_op jit(solution)/shard_map/ppermute | solution.py:258
  40.9 6.1 %collective-permute-start.19 = (bf16[256,128]{1,0:T(8,128)(2,1)S(1)}, bf16[256,128]{1,0:T(8,128)(2,1)S(1)}, u32[]{:S(2)}, u32[]{:S(2)}) collective-permute-start(bf16[256,128]{1,0:T(8,128)(2,1)S(1)} %shard_map.68.refs_0_), channel_id=1, source_target_pairs={{0,6},{1,7},{2,4},{3,5},{4,2},{5,3},{6,0},{7,1},{8,14},{9,15},{10,... | collective-permute-start | bytes 196616 | tf_op jit(solution)/shard_map/ppermute | solution.py:258
  47.0 13.7 %collective-permute-start.30 = (bf16[3,256,128]{2,1,0:T(8,128)(2,1)S(1)}, bf16[3,256,128]{2,1,0:T(8,128)(2,1)S(1)}, u32[]{:S(2)}, u32[]{:S(2)}) collective-permute-start(bf16[3,256,128]{2,1,0:T(8,128)(2,1)S(1)} %get-tuple-element.49), channel_id=1, source_target_pairs={{0,8},{8,0},{16,24},{24,16},{1,9},{9,1},{17,25},{25,17},{2,10},{10... | collective-permute-start | bytes 589832 | tf_op jit(solution)/shard_map/ppermute | solution.py:258
  48.6 4.9 %collective-permute-start.29 = (bf16[256,128]{1,0:T(8,128)(2,1)S(1)}, bf16[256,128]{1,0:T(8,128)(2,1)S(1)}, u32[]{:S(2)}, u32[]{:S(2)}) collective-permute-start(bf16[256,128]{1,0:T(8,128)(2,1)S(1)} %shard_map.68.refs_0_), channel_id=1, source_target_pairs={{0,8},{8,0},{16,24},{24,16},{1,9},{9,1},{17,25},{25,17},{2,10},{10... | collective-permute-start | bytes 196616 | tf_op jit(solution)/shard_map/ppermute | solution.py:258
  49.1 11.3 %collective-permute-start.25 = (bf16[256,128]{1,0:T(8,128)(2,1)S(1)}, bf16[256,128]{1,0:T(8,128)(2,1)S(1)}, u32[]{:S(2)}, u32[]{:S(2)}) collective-permute-start(bf16[256,128]{1,0:T(8,128)(2,1)S(1)} %shard_map.68.refs_0_), channel_id=1, source_target_pairs={{0,16},{8,24},{16,0},{24,8},{1,17},{9,25},{17,1},{25,9},{2,18},{10... | collective-permute-start | bytes 196616 | tf_op jit(solution)/shard_map/ppermute | solution.py:258
  49.6 11.1 %collective-permute-start.21 = (bf16[256,128]{1,0:T(8,128)(2,1)S(1)}, bf16[256,128]{1,0:T(8,128)(2,1)S(1)}, u32[]{:S(2)}, u32[]{:S(2)}) collective-permute-start(bf16[256,128]{1,0:T(8,128)(2,1)S(1)} %shard_map.68.refs_0_), channel_id=1, source_target_pairs={{0,24},{8,16},{16,8},{24,0},{1,25},{9,17},{17,9},{25,1},{2,26},{10... | collective-permute-start | bytes 196616 | tf_op jit(solution)/shard_map/ppermute | solution.py:258
  52.1 34.1 %collective-permute-start.28 = (bf16[256,1024]{1,0:T(8,128)(2,1)S(1)}, bf16[256,1024]{1,0:T(8,128)(2,1)S(1)}, u32[]{:S(2)}, u32[]{:S(2)}) collective-permute-start(bf16[256,1024]{1,0:T(8,128)(2,1)S(1)} %get-tuple-element.29.batch), channel_id=1, source_target_pairs={{0,16},{8,24},{16,0},{24,8},{1,17},{9,25},{17,1},{25,9},{2,18},{10... | collective-permute-start | bytes 1572872 | tf_op jit(solution)/shard_map/ppermute | solution.py:258
  53.5 29.7 %collective-permute-start.26 = (bf16[3,256,128]{2,1,0:T(8,128)(2,1)S(1)}, bf16[3,256,128]{2,1,0:T(8,128)(2,1)S(1)}, u32[]{:S(2)}, u32[]{:S(2)}) collective-permute-start(bf16[3,256,128]{2,1,0:T(8,128)(2,1)S(1)} %get-tuple-element.49), channel_id=1, source_target_pairs={{0,16},{8,24},{16,0},{24,8},{1,17},{9,25},{17,1},{25,9},{2,18},{10... | collective-permute-start | bytes 589832 | tf_op jit(solution)/shard_map/ppermute | solution.py:258
  60.4 26.8 %collective-permute-start.24 = (bf16[256,1024]{1,0:T(8,128)(2,1)S(1)}, bf16[256,1024]{1,0:T(8,128)(2,1)S(1)}, u32[]{:S(2)}, u32[]{:S(2)}) collective-permute-start(bf16[256,1024]{1,0:T(8,128)(2,1)S(1)} %get-tuple-element.29.batch), channel_id=1, source_target_pairs={{0,24},{8,16},{16,8},{24,0},{1,25},{9,17},{17,9},{25,1},{2,26},{10... | collective-permute-start | bytes 1572872 | tf_op jit(solution)/shard_map/ppermute | solution.py:258
  60.8 23.1 %collective-permute-start.20 = (bf16[4,256,128]{2,1,0:T(8,128)(2,1)S(1)}, bf16[4,256,128]{2,1,0:T(8,128)(2,1)S(1)}, u32[]{:S(2)}, u32[]{:S(2)}) collective-permute-start(bf16[4,256,128]{2,1,0:T(8,128)(2,1)S(1)} %get-tuple-element.47.half), channel_id=1, source_target_pairs={{0,1},{1,0},{2,3},{3,2},{4,5},{5,4},{6,7},{7,6},{8,9},{9,8},{10,11... | collective-permute-start | bytes 786440 | tf_op jit(solution)/shard_map/ppermute | solution.py:258
  60.8 22.5 %collective-permute-start.22 = (bf16[3,256,128]{2,1,0:T(8,128)(2,1)S(1)}, bf16[3,256,128]{2,1,0:T(8,128)(2,1)S(1)}, u32[]{:S(2)}, u32[]{:S(2)}) collective-permute-start(bf16[3,256,128]{2,1,0:T(8,128)(2,1)S(1)} %get-tuple-element.49), channel_id=1, source_target_pairs={{0,24},{8,16},{16,8},{24,0},{1,25},{9,17},{17,9},{25,1},{2,26},{10... | collective-permute-start | bytes 589832 | tf_op jit(solution)/shard_map/ppermute | solution.py:258
  (9 other events, 29.6 us)
